TPU v7x, 32 devices: a whole 2x2x4 slice. The times are simulated.
32 devices in a mesh: tm: 32 (over z, y, x, core).
Axes of the slice: x: 2, y: 2, z: 4, core: 2. Of those that a mesh axis runs over, the one named last changes fastest.
Arguments:
- initial: float32 [2, 64, 64], replicated, may hold values from 0 to 0.6
- coarse_guess: float32 [32, 2, 64, 64], P('tm'), may hold values from 0 to 0.6
- feed_rate: float32 [64, 64], replicated, may hold values from 0.02 to 0.08
- kill_rate: float32 [64, 64], replicated, may hold values from 0.03 to 0.07
Outputs:
- trajectory: float32 [128, 2, 64, 64], P('tm')
- c_residual: float32 [32, 2, 64, 64], P('tm')
- group_coarse: float32 [32, 2, 64, 64], P('tm')
- level_defect: float32 [32, 2, 64, 64], P('tm')
All inputs are finite; a program needn't handle non-finite values.
Results may differ from a plain program's by a relative error of at most 0.0004.
Values sent between devices are 32-bit elements; how exact they have to be, the bound alone decides.
A program may use at most 64 MiB of HBM per device.

v0:
```python
import jax
import jax.numpy as jnp
from jax import lax
from jax.sharding import PartitionSpec as P

STEPS_DEV = 4
GROUP = 16


diffusion = (0.2, 0.1)
interval_time = 0.03125
highest = lax.Precision.HIGHEST


def shifted_2(block, axis, distance):
    devices = range(lax.axis_size(axis))
    route = [(i - distance, i) for i in devices if i - distance in devices]
    return lax.ppermute(block, axis, route)


def partner_2(block, axis, apart):
    count = lax.axis_size(axis)
    route = []
    for low in range(count):
        high = low | 1 << apart
        if high != low and high < count:
            route += [(low, high), (high, low)]
    return lax.ppermute(block, axis, route)


def cosine_basis(length):
    positions = jnp.arange(length, dtype=jnp.float32)
    angles = jnp.pi * (positions[:, None] + 0.5) * positions[None, :] / length
    weight = jnp.where(positions == 0, jnp.sqrt(1.0 / length), jnp.sqrt(2.0 / length))
    return jnp.cos(angles) * weight[None, :]


def eigen_values(length):
    positions = jnp.arange(length, dtype=jnp.float32)
    return -4.0 * jnp.sin(jnp.pi * positions / (2.0 * length)) ** 2


def make_tables(rows_first, rows_second):
    spectrum = eigen_values(rows_first)[:, None] + eigen_values(rows_second)[None, :]
    return (cosine_basis(rows_first), cosine_basis(rows_second), spectrum)


def advance(fields, feed_rate, kill_rate, time_step, tables):
    basis_rows, basis_cols, spectrum = tables
    substrate = fields[..., 0, :, :]
    catalyst = fields[..., 1, :, :]
    uptake = substrate * catalyst * catalyst
    substrate_new = substrate + time_step * (feed_rate * (1.0 - substrate) - uptake)
    catalyst_new = catalyst + time_step * (uptake - (feed_rate + kill_rate) * catalyst)
    reacted = jnp.stack([substrate_new, catalyst_new], axis=-3)
    spectral = jnp.matmul(
        jnp.matmul(basis_rows.T, reacted, precision=highest), basis_cols, precision=highest
    )
    diff_rates = jnp.array(diffusion, dtype=jnp.float32)
    spectral = spectral / (1.0 - time_step * diff_rates[:, None, None] * spectrum)
    return jnp.matmul(
        jnp.matmul(basis_rows, spectral, precision=highest), basis_cols.T, precision=highest
    )


def march(start_state, feed_rate, kill_rate, time_step, tables, count_steps):

    def turn(fields, unused):
        fields = advance(fields, feed_rate, kill_rate, time_step, tables)
        return (fields, fields)

    finished, visited = lax.scan(turn, start_state, None, length=count_steps)
    return (finished, visited)


def shards(initial, coarse_guess, feed_rate, kill_rate):
    tables = make_tables(initial.shape[1], initial.shape[2])
    fine_step = interval_time / STEPS_DEV
    coarse_step = interval_time * GROUP
    devices = lax.axis_size("tm")
    groups = devices // GROUP
    position = lax.axis_index("tm")
    leading = position == 0
    member = position % GROUP
    group_id = position // GROUP
    start_count = jnp.zeros((), jnp.int32)

    def evolve(fields, time_step):
        return advance(fields, feed_rate, kill_rate, time_step, tables)

    own_guess = coarse_guess[0]
    incoming = shifted_2(own_guess, "tm", 1)
    incoming = jnp.where(leading, initial, incoming)
    relaxed, unused = march(incoming, feed_rate, kill_rate, fine_step, tables, STEPS_DEV)
    shifted = shifted_2(relaxed, "tm", 1)
    shifted = jnp.where(leading, initial, shifted)
    arrived, unused = march(shifted, feed_rate, kill_rate, fine_step, tables, STEPS_DEV)
    c_residual = arrived - relaxed
    level_rhs = arrived - evolve(shifted, interval_time)
    windows = (shifted[None], level_rhs[None])
    for level_bit in range(GROUP.bit_length() - 1):
        partner = partner_2(windows, "tm", level_bit)
        is_lower = position >> level_bit & 1 == 0
        windows = tuple(
            (
                jnp.where(
                    is_lower,
                    jnp.concatenate([own_part, their_part], 0),
                    jnp.concatenate([their_part, own_part], 0),
                )
                for own_part, their_part in zip(windows, partner)
            )
        )
    starts, right_sides = windows
    group_start = starts[0]

    def level_turn(fields, right_side):
        fields = evolve(fields, interval_time) + right_side
        return (fields, None)

    last_point, unused = lax.scan(level_turn, group_start, right_sides[:-1])
    closing = evolve(last_point, interval_time) + right_sides[-1]
    coarse_term = closing - evolve(group_start, coarse_step)
    flattened = coarse_term.reshape((-1, coarse_term.shape[-1]))
    height = flattened.shape[0] // GROUP
    own_piece = lax.dynamic_slice_in_dim(flattened, member * height, height, 0)
    gathered = lax.all_gather(own_piece, "tm", axis=0, tiled=True)
    coarse_rhs = gathered.reshape((groups,) + initial.shape)

    def coarse_turn(state_pack, right_side):
        fields, earlier, mine_value, counter = state_pack
        fields = evolve(fields, coarse_step) + right_side
        earlier = jnp.where(counter == group_id - 1, fields, earlier)
        mine_value = jnp.where(counter == group_id, fields, mine_value)
        return ((fields, earlier, mine_value, counter + 1), None)

    packed, unused = lax.scan(
        coarse_turn, (initial, initial, initial, start_count), coarse_rhs, unroll=4
    )
    earlier = packed[1]
    mine_value = packed[2]

    def replay(state_pack, right_side):
        fields, chosen, counter = state_pack
        fields = evolve(fields, interval_time) + right_side
        chosen = jnp.where(counter == member, fields, chosen)
        return ((fields, chosen, counter + 1), None)

    replayed, unused = lax.scan(replay, (earlier, mine_value, start_count), right_sides)
    finishing = replayed[0]
    corrected = jnp.where(member == GROUP - 1, mine_value, replayed[1])
    level_defect = jnp.where(
        member == GROUP - 1, finishing - mine_value, jnp.zeros_like(mine_value)
    )
    prior_state = shifted_2(corrected, "tm", 1)
    prior_state = jnp.where(leading, initial, prior_state)
    unused, interior = march(prior_state, feed_rate, kill_rate, fine_step, tables, STEPS_DEV - 1)
    trajectory = jnp.concatenate([interior, corrected[None]], axis=0)
    return (trajectory, c_residual[None], mine_value[None], level_defect[None])


def solution(mesh):
    in_specs = (P(), P("tm", None, None, None), P(), P())
    out_specs = (
        P("tm", None, None, None),
        P("tm", None, None, None),
        P("tm", None, None, None),
        P("tm", None, None, None),
    )
    return jax.shard_map(shards, mesh=mesh, in_specs=in_specs, out_specs=out_specs, check_vma=False)
```

profile of v0, /device:TPU:0, one launch (start us, length us, event | category | flops | bytes accessed | tf_op | source)
XLA Modules:
  0.0 182.6 jit_solution(10836515565205340700)
XLA Ops:
  0.6 2.4 %collective-permute-start = (f32[2,64,64]{2,1,0:T(8,128)}, f32[2,64,64]{2,1,0:T(8,128)S(1)}, u32[]{:S(2)}, u32[]{:S(2)}) collective-permute-start(f32[2,64,64]{2,1,0:T(8,128)} %bitcast.498), channel_id=1, source_target_pairs={{0,1},{1,2},{2,3},{3,4},{4,5},{5,6},{6,7},{7,8},{8,9},{9,10},{10,1... | collective-permute-start | bytes 98312 | tf_op jit(solution)/shard_map/ppermute | solution.py:18
  3.1 0.8 fusion.192
  3.9 0.4 fusion.160
  5.4 6.7 %while.87 = (s32[]{:T(128)}, f32[2,64,64]{2,1,0:T(8,128)S(1)}, f32[64,64]{1,0:T(8,128)S(1)}, f32[1,64,64]{2,1,0:T(8,128)S(1)}, f32[64]{0:T(128)S(1)}, /*index=5*...) while((s32[]{:T(128)}, f32[2,64,64]{2,1,0:T(8,128)S(1)}, ...), condition=%wide.region_1.2_spmd.clone.clone.clone, body=%wide.region_0.1_spmd.sunk.clone.clone.clone.sunk | while | flops 25296896 | bytes 395621 | solution.py:72
  12.2 4.5 %collective-permute-start.1 = (f32[2,64,64]{2,1,0:T(8,128)S(1)}, f32[2,64,64]{2,1,0:T(8,128)S(1)}, u32[]{:S(2)}, u32[]{:S(2)}) collective-permute-start(f32[2,64,64]{2,1,0:T(8,128)S(1)} %get-tuple-element.754), channel_id=1, source_target_pairs={{0,1},{1,2},{2,3},{3,4},{4,5},{5,6},{6,7},{7,8},{8,9},{9,10},{10,1... | collective-permute-start | bytes 98312 | tf_op jit(solution)/shard_map/ppermute | solution.py:18
  16.8 0.7 collective-permute-done.1
  17.7 2.6 %collective-permute-start.2 = (f32[1,2,64,64]{3,2,1,0:T(8,128)S(1)}, f32[1,2,64,64]{3,2,1,0:T(8,128)S(1)}, u32[]{:S(2)}, u32[]{:S(2)}) collective-permute-start(f32[1,2,64,64]{3,2,1,0:T(8,128)S(1)} %bitcast.486), channel_id=1, source_target_pairs={{0,1},{1,0},{2,3},{3,2},{4,5},{5,4},{6,7},{7,6},{8,9},{9,8},{10,11... | collective-permute-start | bytes 98312 | tf_op jit(solution)/shard_map/ppermute | solution.py:28
  20.3 6.8 %while.88 = (s32[]{:T(128)}, f32[2,64,64]{2,1,0:T(8,128)S(1)}, f32[64,64]{1,0:T(8,128)S(1)}, f32[1,64,64]{2,1,0:T(8,128)S(1)}, f32[64]{0:T(128)S(1)}, /*index=5*...) while((s32[]{:T(128)}, f32[2,64,64]{2,1,0:T(8,128)S(1)}, ...), condition=%wide.region_3.4_spmd.clone.clone.clone, body=%wide.region_2.3_spmd.sunk.clone.clone.clone.sunk | while | flops 25296896 | bytes 395621 | solution.py:72
  27.1 0.4 fusion.164
  27.6 0.6 copy-done.7
  29.4 0.6 collective-permute-start.6
  30.1 2.4 %collective-permute-start.3 = (f32[2,2,64,64]{3,2,1,0:T(8,128)S(1)}, f32[2,2,64,64]{3,2,1,0:T(8,128)S(1)}, u32[]{:S(2)}, u32[]{:S(2)}) collective-permute-start(f32[2,2,64,64]{3,2,1,0:T(8,128)S(1)} %maximum_select_fusion.6), channel_id=1, source_target_pairs={{0,2},{2,0},{1,3},{3,1},{4,6},{6,4},{5,7},{7,5},{8,10},{10,8},{9,1... | collective-permute-start | bytes 196616 | tf_op jit(solution)/shard_map/ppermute | solution.py:28
  32.5 1.1 collective-permute-start.7
  33.6 3.2 %collective-permute-done.3 = f32[2,2,64,64]{3,2,1,0:T(8,128)S(1)} collective-permute-done((f32[2,2,64,64]{3,2,1,0:T(8,128)S(1)}, f32[2,2,64,64]{3,2,1,0:T(8,128)S(1)}, u32[]{:S(2)}, u32[]{:S(2)}) %collective-permute-start.3) | collective-permute-done | bytes 65568 | tf_op jit(solution)/shard_map/ppermute | solution.py:28
  36.9 3.8 %collective-permute-start.4 = (f32[4,2,64,64]{3,2,1,0:T(8,128)S(1)}, f32[4,2,64,64]{3,2,1,0:T(8,128)S(1)}, u32[]{:S(2)}, u32[]{:S(2)}) collective-permute-start(f32[4,2,64,64]{3,2,1,0:T(8,128)S(1)} %maximum_select_fusion.4), channel_id=1, source_target_pairs={{0,4},{4,0},{1,5},{5,1},{2,6},{6,2},{3,7},{7,3},{8,12},{12,8},{9,1... | collective-permute-start | bytes 393224 | tf_op jit(solution)/shard_map/ppermute | solution.py:28
  41.2 1.8 collective-permute-start.8
  43.0 4.8 %collective-permute-done.4 = f32[4,2,64,64]{3,2,1,0:T(8,128)S(1)} collective-permute-done((f32[4,2,64,64]{3,2,1,0:T(8,128)S(1)}, f32[4,2,64,64]{3,2,1,0:T(8,128)S(1)}, u32[]{:S(2)}, u32[]{:S(2)}) %collective-permute-start.4) | collective-permute-done | bytes 131104 | tf_op jit(solution)/shard_map/ppermute | solution.py:28
  47.9 3.9 %collective-permute-start.5 = (f32[8,2,64,64]{3,2,1,0:T(8,128)S(1)}, f32[8,2,64,64]{3,2,1,0:T(8,128)S(1)}, u32[]{:S(2)}, u32[]{:S(2)}) collective-permute-start(f32[8,2,64,64]{3,2,1,0:T(8,128)S(1)} %maximum_select_fusion.2), channel_id=1, source_target_pairs={{0,8},{8,0},{1,9},{9,1},{2,10},{10,2},{3,11},{11,3},{4,12},{12,4},... | collective-permute-start | bytes 786440 | tf_op jit(solution)/shard_map/ppermute | solution.py:28
  52.3 3.4 %collective-permute-start.9 = (f32[8,2,64,64]{3,2,1,0:T(8,128)S(1)}, f32[8,2,64,64]{3,2,1,0:T(8,128)S(1)}, u32[]{:S(2)}, u32[]{:S(2)}) collective-permute-start(f32[8,2,64,64]{3,2,1,0:T(8,128)S(1)} %maximum_select_fusion.3), channel_id=1, source_target_pairs={{0,8},{8,0},{1,9},{9,1},{2,10},{10,2},{3,11},{11,3},{4,12},{12,4},... | collective-permute-start | bytes 786440 | tf_op jit(solution)/shard_map/ppermute | solution.py:28
  55.6 9.0 %collective-permute-done.5 = f32[8,2,64,64]{3,2,1,0:T(8,128)S(1)} collective-permute-done((f32[8,2,64,64]{3,2,1,0:T(8,128)S(1)}, f32[8,2,64,64]{3,2,1,0:T(8,128)S(1)}, u32[]{:S(2)}, u32[]{:S(2)}) %collective-permute-start.5) | collective-permute-done | bytes 262176 | tf_op jit(solution)/shard_map/ppermute | solution.py:28
  64.7 6.9 %collective-permute-done.9 = f32[8,2,64,64]{3,2,1,0:T(8,128)S(1)} collective-permute-done((f32[8,2,64,64]{3,2,1,0:T(8,128)S(1)}, f32[8,2,64,64]{3,2,1,0:T(8,128)S(1)}, u32[]{:S(2)}, u32[]{:S(2)}) %collective-permute-start.9) | collective-permute-done | bytes 262176 | tf_op jit(solution)/shard_map/ppermute | solution.py:28
  71.9 0.6 copy-done.8
  72.4 25.4 %while.89 = (s32[]{:T(128)}, f32[2,64,64]{2,1,0:T(8,128)S(1)}, f32[64,64]{1,0:T(8,128)S(1)}, f32[1,64,64]{2,1,0:T(8,128)S(1)}, f32[15,2,64,64]{3,2,1,0:T(8,128)S...) while((s32[]{:T(128)}, f32[2,64,64]{2,1,0:T(8,128)S(1)}, ...), condition=%wide.region_5.6_spmd.clone.clone.clone, body=%wide.region_4.5_spmd.sunk.clone.clone.clone.sunk | while | flops 25305088 | bytes 428409 | solution.py:121
  73.7 0.4 convolution_add_fusion.5
  75.4 0.4 convolution_add_fusion.5
  77.1 0.4 convolution_add_fusion.5
  78.8 0.4 convolution_add_fusion.5
  80.5 0.4 convolution_add_fusion.5
  82.2 0.4 convolution_add_fusion.5
  83.9 0.4 convolution_add_fusion.5
  85.6 0.4 convolution_add_fusion.5
  87.2 0.4 convolution_add_fusion.5
  88.9 0.4 convolution_add_fusion.5
  90.6 0.4 convolution_add_fusion.5
  92.3 0.4 convolution_add_fusion.5
  94.0 0.4 convolution_add_fusion.5
  97.9 0.4 fusion.172
  99.1 0.4 fusion.168
  101.2 41.0 %all_gather.3 = f32[256,64]{1,0:T(8,128)S(1)} all-gather(f32[8,64]{1,0:T(8,128)S(1)} %constant_dynamic-slice_fusion), channel_id=1, replica_groups=mesh['tm'=32] {'tm'}, dimensions={0}, use_global_device_ids=true | all-gather | bytes 67584 | tf_op jit(solution)/shard_map/all_gather | solution.py:127
  142.6 0.4 fusion.176
  143.9 0.4 select_select_fusion
  144.4 0.7 copy-done.5
  145.0 27.5 %while.90 = (s32[]{:T(128)}, f32[2,64,64]{2,1,0:T(8,128)S(1)}, f32[2,64,64]{2,1,0:T(8,128)S(1)}, f32[64,64]{1,0:T(8,128)S(1)}, f32[1,64,64]{2,1,0:T(8,128)S(1)},...) while((s32[]{:T(128)}, f32[2,64,64]{2,1,0:T(8,128)S(1)}, ...), condition=%wide.region_7.8_spmd.clone.clone.clone, body=%wide.region_6.7_spmd.sunk.clone.clone.clone.sunk | while | flops 25313284 | bytes 493971 | solution.py:149
  146.3 0.4 broadcast_select_fusion.6
  148.0 0.4 broadcast_select_fusion.6
  149.7 0.4 broadcast_select_fusion.6
  151.4 0.4 broadcast_select_fusion.6
  153.2 0.4 broadcast_select_fusion.6
  154.9 0.4 broadcast_select_fusion.6
  156.6 0.4 broadcast_select_fusion.6
  158.3 0.4 broadcast_select_fusion.6
  160.0 0.4 broadcast_select_fusion.6
  161.8 0.4 broadcast_select_fusion.6
  163.5 0.4 broadcast_select_fusion.6
  165.2 0.4 broadcast_select_fusion.6
  166.9 0.4 broadcast_select_fusion.6
  168.6 0.4 broadcast_select_fusion.6
  170.3 0.4 broadcast_select_fusion.6
  172.1 0.4 broadcast_select_fusion.6
  172.5 0.6 select_bitcast_fusion
  173.2 2.4 %collective-permute-start.10 = (f32[2,64,64]{2,1,0:T(8,128)S(1)}, f32[2,64,64]{2,1,0:T(8,128)S(1)}, u32[]{:S(2)}, u32[]{:S(2)}) collective-permute-start(f32[2,64,64]{2,1,0:T(8,128)S(1)} %get-tuple-element.1219), channel_id=1, source_target_pairs={{0,1},{1,2},{2,3},{3,4},{4,5},{5,6},{6,7},{7,8},{8,9},{9,10},{10,1... | collective-permute-start | bytes 98312 | tf_op jit(solution)/shard_map/ppermute | solution.py:18
  175.5 0.6 subtract_bitcast_fusion
  176.8 5.1 %while.91 = (s32[]{:T(128)}, f32[2,64,64]{2,1,0:T(8,128)S(1)}, f32[3,2,64,64]{3,2,1,0:T(8,128)S(1)}, f32[64,64]{1,0:T(8,128)S(1)}, f32[1,64,64]{2,1,0:T(8,128)S(...) while((s32[]{:T(128)}, f32[2,64,64]{2,1,0:T(8,128)S(1)}, ...), condition=%wide.region_9.10_spmd.clone.clone.clone, body=%wide.region_8.9_spmd.sunk.clone.clone.clone.sunk | while | flops 25296896 | bytes 527225 | solution.py:72
  181.9 0.7 pad_maximum_fusion
  (291 shorter events, 65.4 us)
Async XLA Ops:
  0.6 3.8 %collective-permute-start = (f32[2,64,64]{2,1,0:T(8,128)}, f32[2,64,64]{2,1,0:T(8,128)S(1)}, u32[]{:S(2)}, u32[]{:S(2)}) collective-permute-start(f32[2,64,64]{2,1,0:T(8,128)} %bitcast.498), channel_id=1, source_target_pairs={{0,1},{1,2},{2,3},{3,4},{4,5},{5,6},{6,7},{7,8},{8,9},{9,10},{10,1... | collective-permute-start | bytes 98312 | tf_op jit(solution)/shard_map/ppermute | solution.py:18
  3.9 0.8 copy-start.1
  4.4 0.8 copy-start
  4.8 0.7 copy-start.10
  12.2 5.4 %collective-permute-start.1 = (f32[2,64,64]{2,1,0:T(8,128)S(1)}, f32[2,64,64]{2,1,0:T(8,128)S(1)}, u32[]{:S(2)}, u32[]{:S(2)}) collective-permute-start(f32[2,64,64]{2,1,0:T(8,128)S(1)} %get-tuple-element.754), channel_id=1, source_target_pairs={{0,1},{1,2},{2,3},{3,4},{4,5},{5,6},{6,7},{7,8},{8,9},{9,10},{10,1... | collective-permute-start | bytes 98312 | tf_op jit(solution)/shard_map/ppermute | solution.py:18
  17.6 2.7 %copy-start.9 = (f32[2]{0:T(128)S(1)}, f32[2]{0:T(128)}, u32[]{:S(2)}) copy-start(f32[2]{0:T(128)} %constant.628) | copy-start | bytes 28
  17.7 12.4 %collective-permute-start.2 = (f32[1,2,64,64]{3,2,1,0:T(8,128)S(1)}, f32[1,2,64,64]{3,2,1,0:T(8,128)S(1)}, u32[]{:S(2)}, u32[]{:S(2)}) collective-permute-start(f32[1,2,64,64]{3,2,1,0:T(8,128)S(1)} %bitcast.486), channel_id=1, source_target_pairs={{0,1},{1,0},{2,3},{3,2},{4,5},{5,4},{6,7},{7,6},{8,9},{9,8},{10,11... | collective-permute-start | bytes 98312 | tf_op jit(solution)/shard_map/ppermute | solution.py:28
  27.6 0.7 copy-start.7
  29.4 3.1 %collective-permute-start.6 = (f32[1,2,64,64]{3,2,1,0:T(8,128)S(1)}, f32[1,2,64,64]{3,2,1,0:T(8,128)S(1)}, u32[]{:S(2)}, u32[]{:S(2)}) collective-permute-start(f32[1,2,64,64]{3,2,1,0:T(8,128)S(1)} %fusion.158), channel_id=1, source_target_pairs={{0,1},{1,0},{2,3},{3,2},{4,5},{5,4},{6,7},{7,6},{8,9},{9,8},{10,11... | collective-permute-start | bytes 98312 | tf_op jit(solution)/shard_map/ppermute | solution.py:28
  30.1 6.8 %collective-permute-start.3 = (f32[2,2,64,64]{3,2,1,0:T(8,128)S(1)}, f32[2,2,64,64]{3,2,1,0:T(8,128)S(1)}, u32[]{:S(2)}, u32[]{:S(2)}) collective-permute-start(f32[2,2,64,64]{3,2,1,0:T(8,128)S(1)} %maximum_select_fusion.6), channel_id=1, source_target_pairs={{0,2},{2,0},{1,3},{3,1},{4,6},{6,4},{5,7},{7,5},{8,10},{10,8},{9,1... | collective-permute-start | bytes 196616 | tf_op jit(solution)/shard_map/ppermute | solution.py:28
  32.5 8.6 %collective-permute-start.7 = (f32[2,2,64,64]{3,2,1,0:T(8,128)S(1)}, f32[2,2,64,64]{3,2,1,0:T(8,128)S(1)}, u32[]{:S(2)}, u32[]{:S(2)}) collective-permute-start(f32[2,2,64,64]{3,2,1,0:T(8,128)S(1)} %maximum_select_fusion.7), channel_id=1, source_target_pairs={{0,2},{2,0},{1,3},{3,1},{4,6},{6,4},{5,7},{7,5},{8,10},{10,8},{9,1... | collective-permute-start | bytes 196616 | tf_op jit(solution)/shard_map/ppermute | solution.py:28
  36.9 3.8 %copy-start.6 = (f32[2]{0:T(128)S(1)}, f32[2]{0:T(128)}, u32[]{:S(2)}) copy-start(f32[2]{0:T(128)} %constant.228) | copy-start | bytes 28
  36.9 10.9 %collective-permute-start.4 = (f32[4,2,64,64]{3,2,1,0:T(8,128)S(1)}, f32[4,2,64,64]{3,2,1,0:T(8,128)S(1)}, u32[]{:S(2)}, u32[]{:S(2)}) collective-permute-start(f32[4,2,64,64]{3,2,1,0:T(8,128)S(1)} %maximum_select_fusion.4), channel_id=1, source_target_pairs={{0,4},{4,0},{1,5},{5,1},{2,6},{6,2},{3,7},{7,3},{8,12},{12,8},{9,1... | collective-permute-start | bytes 393224 | tf_op jit(solution)/shard_map/ppermute | solution.py:28
  41.2 11.0 %collective-permute-start.8 = (f32[4,2,64,64]{3,2,1,0:T(8,128)S(1)}, f32[4,2,64,64]{3,2,1,0:T(8,128)S(1)}, u32[]{:S(2)}, u32[]{:S(2)}) collective-permute-start(f32[4,2,64,64]{3,2,1,0:T(8,128)S(1)} %maximum_select_fusion.5), channel_id=1, source_target_pairs={{0,4},{4,0},{1,5},{5,1},{2,6},{6,2},{3,7},{7,3},{8,12},{12,8},{9,1... | collective-permute-start | bytes 393224 | tf_op jit(solution)/shard_map/ppermute | solution.py:28
  47.9 16.7 %collective-permute-start.5 = (f32[8,2,64,64]{3,2,1,0:T(8,128)S(1)}, f32[8,2,64,64]{3,2,1,0:T(8,128)S(1)}, u32[]{:S(2)}, u32[]{:S(2)}) collective-permute-start(f32[8,2,64,64]{3,2,1,0:T(8,128)S(1)} %maximum_select_fusion.2), channel_id=1, source_target_pairs={{0,8},{8,0},{1,9},{9,1},{2,10},{10,2},{3,11},{11,3},{4,12},{12,4},... | collective-permute-start | bytes 786440 | tf_op jit(solution)/shard_map/ppermute | solution.py:28
  52.3 19.4 %collective-permute-start.9 = (f32[8,2,64,64]{3,2,1,0:T(8,128)S(1)}, f32[8,2,64,64]{3,2,1,0:T(8,128)S(1)}, u32[]{:S(2)}, u32[]{:S(2)}) collective-permute-start(f32[8,2,64,64]{3,2,1,0:T(8,128)S(1)} %maximum_select_fusion.3), channel_id=1, source_target_pairs={{0,8},{8,0},{1,9},{9,1},{2,10},{10,2},{3,11},{11,3},{4,12},{12,4},... | collective-permute-start | bytes 786440 | tf_op jit(solution)/shard_map/ppermute | solution.py:28
  71.8 0.7 copy-start.8
  144.3 28.2 %copy-start.2 = (f32[2,64,64]{2,1,0:T(8,128)}, f32[2,64,64]{2,1,0:T(8,128)S(1)}, u32[]{:S(2)}) copy-start(f32[2,64,64]{2,1,0:T(8,128)S(1)} %get-tuple-element.1589) | copy-start | bytes 98308
  144.3 0.7 copy-start.5
  173.1 3.3 %copy-start.3 = (f32[3,2,64,64]{3,2,1,0:T(8,128)S(1)}, f32[3,2,64,64]{3,2,1,0:T(8,128)}, u32[]{:S(2)}) copy-start(f32[3,2,64,64]{3,2,1,0:T(8,128)} %custom-call) | copy-start | bytes 294916
  173.2 3.3 %collective-permute-start.10 = (f32[2,64,64]{2,1,0:T(8,128)S(1)}, f32[2,64,64]{2,1,0:T(8,128)S(1)}, u32[]{:S(2)}, u32[]{:S(2)}) collective-permute-start(f32[2,64,64]{2,1,0:T(8,128)S(1)} %get-tuple-element.1219), channel_id=1, source_target_pairs={{0,1},{1,2},{2,3},{3,4},{4,5},{5,6},{6,7},{7,8},{8,9},{9,10},{10,1... | collective-permute-start | bytes 98312 | tf_op jit(solution)/shard_map/ppermute | solution.py:18
  176.2 0.7 copy-start.4
where the time goes:
time: 183 us
  matrix products  73.2 us (40%)
  blocking collectives  41 us (22%)
  starting transfers between devices  29 us (16%)
  waiting for transfers between devices  24.9 us (14%)
  other arithmetic  7.27 us (4%)
  local copies, waits for them, and re-layouts  3.7 us (2%)
  loops' own time  2.28 us (1%)
    all_gather x1, blocking collectives, shards(): gathered = lax.all_gather(own_piece, 'tm', axis=0, tiled=True)  41 us
    ppermute x8, waiting for transfers between devices, partner_2(): return lax.ppermute(block, axis, route)  23.9 us
    ppermute x8, starting transfers between devices, partner_2(): return lax.ppermute(block, axis, route)  19.7 us
    dot_general x47, matrix products, advance(): jnp.matmul(jnp.matmul(basis_rows, spectral, precision=highest), basis_col...  18.9 us
    dot_general x47, matrix products, advance(): jnp.matmul(basis_rows.T, reacted, precision=highest)  18.5 us
    dot_general x47, matrix products, advance(): jnp.matmul(jnp.matmul(basis_rows.T, reacted, precision=highest), basis_co...  18.5 us
    dot_general x47, matrix products, advance(): jnp.matmul(basis_rows, spectral, precision=highest)  17.4 us
    ppermute x3, starting transfers between devices, shifted_2(): return lax.ppermute(block, axis, route)  9.26 us
  transfers between devices with their start and end apart: 11, of which 6 were waited for; matrix products, arithmetic and copies ran while one was open for 6% of the time, Pallas kernels for 0%

commit v1 on v0

v1 whole, which is shorter than its diff:
```python
import functools

import jax
import jax.numpy as jnp
import ml_dtypes
import numpy as np
from jax import lax
from jax.experimental import pallas as pl
from jax.experimental.pallas import tpu as pltpu
from jax.sharding import PartitionSpec as P

STEPS_DEV = 4
GROUP = 16

diffusion = (0.2, 0.1)
interval_time = 0.03125
MESH = pl.DeviceIdType.MESH
single = np.float32


def cosine_basis(length):
    positions = np.arange(length, dtype=single)
    angles = single(np.pi) * (positions[:, None] + single(0.5)) * positions[None, :] / single(length)
    weight = np.where(positions == 0, np.sqrt(single(1.0 / length)), np.sqrt(single(2.0 / length)))
    return (np.cos(angles) * weight[None, :].astype(single)).astype(single)


def eigen_values(length):
    positions = np.arange(length, dtype=single)
    waves = np.sin(single(np.pi) * positions / single(2.0 * length))
    return (single(-4.0) * waves * waves).astype(single)


def halves(matrix):
    high = matrix.astype(ml_dtypes.bfloat16)
    low = (matrix - high.astype(np.float64)).astype(ml_dtypes.bfloat16)
    return high, low


def factors(rows, cols, time_step, rate, rank):
    basis_rows = cosine_basis(rows).astype(np.float64)
    basis_cols = cosine_basis(cols).astype(np.float64)
    spectrum = eigen_values(rows).astype(np.float64)[:, None] + eigen_values(cols).astype(np.float64)[None, :]
    factor = 1.0 / (1.0 - time_step * rate * spectrum)
    left, sizes, right = np.linalg.svd(factor)
    if rank is None:
        rank = 1
        while np.abs(factor - (left[:, :rank] * sizes[:rank]) @ right[:rank]).max() > 2.0**-26:
            rank += 1
        return rank
    left = left[:, :rank] * np.sqrt(sizes[:rank])
    right = right[:rank].T * np.sqrt(sizes[:rank])
    scale = left[0, 0]
    left[:, 0] /= scale
    right[:, 0] *= scale
    firsts = [basis_rows @ np.diag(left[:, k]) @ basis_rows.T for k in range(rank)]
    seconds = [basis_cols @ np.diag(right[:, k]) @ basis_cols.T for k in range(rank)]
    firsts[0] = firsts[0] - np.eye(rows)
    seconds[0] = seconds[0] - np.eye(cols)
    return firsts, seconds


@functools.lru_cache(maxsize=None)
def solve_tables(rows, cols, time_step):
    rank = max(factors(rows, cols, time_step, rate, None) for rate in diffusion)
    rank = max(rank, 2)
    species = [factors(rows, cols, time_step, rate, rank) for rate in diffusion]
    short = rank == 2
    blocks_high, blocks_low = [], []
    for k in range(rank):
        block = np.zeros((2 * cols, 2 * cols))
        block[:cols, :cols] = species[0][1][k]
        block[cols:, cols:] = species[1][1][k]
        high, low = halves(block)
        blocks_high.append(high)
        blocks_low.append(low)
    high = np.concatenate(blocks_high, 1)
    right_high = np.concatenate([high, high], 0)
    right_low = np.concatenate(blocks_low[: 1 if short else rank], 1)
    left_high, left_low = [], []
    for k in range(rank):
        high, low = halves(np.concatenate([species[0][0][k], species[1][0][k]], 0))
        left_high.append(high)
        left_low.append(low)
    if short:
        lefts = left_high + left_high[:1] + left_low[:1]
    else:
        lefts = left_high + left_high + left_low
    return right_high, right_low, np.concatenate(lefts, 1)


def kernel(devices, sizes, *refs):
    (initial_ref, guess_ref, feed_ref, kill_ref) = refs[:4]
    table_refs = (refs[4:7], refs[7:10], refs[10:13])
    traj_ref, resid_ref, coarse_ref, defect_ref = refs[13:17]
    (rates, b_buf, s_buf, r_buf, p_buf, e_buf, b_out, r_out, p_out) = refs[17:26]
    (send_b, recv_b, send_s, recv_s, send_r, recv_r, send_p, recv_p, send_e, recv_e) = refs[26:36]
    rows, cols = sizes
    groups = devices // GROUP
    me = lax.axis_index("tm")
    group = me // GROUP
    member = me % GROUP
    base = group * GROUP
    ahead = me + 2
    ahead_group = ahead // GROUP
    ahead_slot = ahead % GROUP
    ahead_valid = ahead < devices

    barrier = pltpu.get_barrier_semaphore()

    def greet(other):
        pl.semaphore_signal(barrier, inc=1, device_id=(other,), device_id_type=MESH)

    def greet_source(k, carry):
        source = base + k - 2

        @pl.when(jnp.logical_and(source >= 0, source != me))
        def _():
            greet(source)

        return carry

    lax.fori_loop(0, GROUP, greet_source, 0)

    @pl.when(me >= 1)
    def _():
        greet(me - 1)

    def greet_group(other, carry):
        greet(other * GROUP + member)
        return carry

    lax.fori_loop(0, group, greet_group, 0)

    left_half = lax.broadcasted_iota(jnp.int32, (rows, 2 * cols), 1) < cols
    fine_step = interval_time / STEPS_DEV
    steps = (fine_step, interval_time, interval_time * GROUP)
    feed = jnp.concatenate([feed_ref[...]] * 2, axis=1)
    kill = jnp.concatenate([kill_ref[...]] * 2, axis=1)
    source_term = jnp.where(left_half, feed, 0.0)
    decay = jnp.where(left_half, feed, feed + kill)
    for level, step in enumerate(steps):
        rates[2 * level] = 1.0 - step * decay
        rates[2 * level + 1] = step * source_term

    def pack(ref):
        return jnp.concatenate([ref[0], ref[1]], axis=1)

    def unpack(ref, index, value):
        ref[index, 0] = value[:, :cols]
        ref[index, 1] = value[:, cols:]

    def split(value):
        high = value.astype(jnp.bfloat16)
        low = (value - high.astype(jnp.float32)).astype(jnp.bfloat16)
        return high, low

    def dot(first, second):
        return jnp.dot(first, second, preferred_element_type=jnp.float32)

    def evolve(level, *states):
        step = steps[level]
        right_high, right_low, lefts = table_refs[level]
        terms = right_high.shape[1] // (2 * cols)
        signed = jnp.where(left_half, -step, step)
        reacted = []
        for state in states:
            swapped = pltpu.roll(state, cols, 1)
            second = jnp.where(left_half, swapped, state)
            uptake = state * swapped * second
            reacted.append(rates[2 * level] * state + rates[2 * level + 1] + signed * uptake)
        main = jnp.concatenate(reacted, 0) if len(reacted) > 1 else reacted[0]
        high, low = split(main)
        wide = dot(jnp.concatenate([high, low], 1), right_high[...])
        narrow = dot(high, right_low[...])
        parts = []
        for k in range(terms):
            part = wide[:, 2 * cols * k : 2 * cols * (k + 1)]
            if 2 * cols * k < right_low.shape[1]:
                part = part + narrow[:, 2 * cols * k : 2 * cols * (k + 1)]
            parts.append(part)
        first = main + parts[0]
        parts[0] = first
        columns = []
        for n in range(len(states)):
            pieces = [part[rows * n : rows * (n + 1)] for part in parts]
            if terms == 2:
                first_high, first_low = split(pieces[0])
                stack = [first_high, pieces[1].astype(jnp.bfloat16), first_low, first_high]
            else:
                pairs = [split(piece) for piece in pieces]
                stack = [a for a, b in pairs] + [b for a, b in pairs] + [a for a, b in pairs]
            columns.append(jnp.concatenate(stack, 0))
        stacked = jnp.concatenate(columns, 1) if len(columns) > 1 else columns[0]
        product = dot(lefts[...], stacked)
        finished = []
        for n in range(len(states)):
            piece = product[:, 2 * cols * n : 2 * cols * (n + 1)]
            small = jnp.where(left_half, piece[:rows], piece[rows:])
            finished.append(first[rows * n : rows * (n + 1)] + small)
        return finished

    start = pack(initial_ref)
    own = pack(guess_ref.at[0])

    def fine_turn(unused, pair):
        return tuple(evolve(0, *pair))

    relaxed, relaxed_zero = lax.fori_loop(0, STEPS_DEV, fine_turn, (own, start))
    r_out[...] = relaxed
    level_relaxed, level_relaxed_zero = evolve(1, relaxed, relaxed_zero)
    arrived, arrived_one = lax.fori_loop(0, STEPS_DEV, fine_turn, (relaxed, relaxed_zero))
    p_out[...] = arrived
    b_out[...] = arrived - level_relaxed

    targets = jnp.where(ahead_valid, GROUP - jnp.where(ahead_group == group, 1, 0), 0)
    targets = targets + jnp.where(me + 1 < devices, 1, 0) + groups - 1 - group

    @pl.when(targets > 0)
    def _():
        pl.semaphore_wait(barrier, targets)

    def remote(source, target, send, recv, other):
        return pltpu.make_async_remote_copy(
            src_ref=source, dst_ref=target, send_sem=send, recv_sem=recv,
            device_id=(other,), device_id_type=MESH,
        )

    def start_copy(i):
        return remote(s_src, s_buf, send_s.at[i], recv_s, ahead_group * GROUP + i)

    s_src = r_out

    def b_copy(i):
        return remote(b_out, b_buf.at[ahead_slot], send_b.at[i], recv_b.at[ahead_slot], ahead_group * GROUP + i)

    sends_start = jnp.logical_and(ahead_valid, ahead_slot == 0)

    def over_group(act):
        def turn(i, carry):
            @pl.when(jnp.logical_and(ahead_valid, ahead_group * GROUP + i != me))
            def _():
                act(i)

            return carry

        lax.fori_loop(0, GROUP, turn, 0)

    @pl.when(sends_start)
    def _():
        def turn(i, carry):
            start_copy(i).start()
            return carry

        lax.fori_loop(0, GROUP, turn, 0)

    over_group(lambda i: b_copy(i).start())
    r_copy = remote(r_out, r_buf, send_r, recv_r, me + 1)
    p_copy = remote(p_out, p_buf, send_p, recv_p, me + 2)

    @pl.when(me + 1 < devices)
    def _():
        r_copy.start()

    @pl.when(ahead_valid)
    def _():
        p_copy.start()

    @pl.when(jnp.logical_and(ahead_valid, ahead_group == group))
    def _():
        b_buf[ahead_slot] = b_out[...]

    @pl.when(group == 0)
    def _():
        (level_start,) = evolve(1, start)
        s_buf[...] = start
        b_buf[0] = relaxed_zero - level_start
        b_buf[1] = arrived_one - level_relaxed_zero

    @pl.when(me == 0)
    def _():
        r_buf[...] = relaxed_zero
        p_buf[...] = relaxed_zero

    @pl.when(me == 1)
    def _():
        p_buf[...] = arrived_one

    @pl.when(group > 0)
    def _():
        remote(r_out, s_buf, send_s.at[0], recv_s, me).wait_recv()

    group_start = s_buf[...]

    def level_turn(k, state):
        source = base + k - 2

        @pl.when(jnp.logical_and(source >= 0, source != me))
        def _():
            remote(b_out, b_buf.at[k], send_b.at[0], recv_b.at[k], me).wait_recv()

        (state,) = evolve(1, state)
        return state + b_buf[k]

    coarse_start, coarse_initial = evolve(2, group_start, start)
    closing = lax.fori_loop(0, GROUP, level_turn, group_start)
    e_buf[group] = closing - coarse_start

    def e_copy(other):
        return remote(e_buf.at[group], e_buf.at[group], send_e.at[other], recv_e.at[group], other * GROUP + member)

    def start_e(other, carry):
        e_copy(other).start()
        return carry

    lax.fori_loop(group + 1, groups, start_e, 0)

    def coarse_turn(other, pair):
        before, image = pair
        remote(e_buf.at[other], e_buf.at[other], send_e.at[0], recv_e.at[other], me).wait_recv()
        after = image + e_buf[other]
        (image,) = evolve(2, after)
        return after, image

    earlier, image = lax.fori_loop(0, group, coarse_turn, (start, coarse_initial))
    mine = image + e_buf[group]

    def replay(k, state):
        (state,) = evolve(1, state)
        return state + b_buf[k]

    prior = lax.fori_loop(0, member, replay, earlier)
    (ending,) = evolve(1, prior)
    ending = ending + b_buf[member]
    point = prior
    for i in range(STEPS_DEV - 1):
        (point,) = evolve(0, point)
        unpack(traj_ref, i, point)
    last = member == GROUP - 1
    unpack(traj_ref, STEPS_DEV - 1, jnp.where(last, mine, ending))
    unpack(coarse_ref, 0, mine)
    unpack(defect_ref, 0, jnp.where(last, ending - mine, 0.0))

    @pl.when(me >= 1)
    def _():
        remote(r_out, r_buf, send_r, recv_r, me).wait_recv()

    @pl.when(me >= 2)
    def _():
        remote(p_out, p_buf, send_p, recv_p, me).wait_recv()

    unpack(resid_ref, 0, p_buf[...] - r_buf[...])

    over_group(lambda i: b_copy(i).wait_send())

    @pl.when(sends_start)
    def _():
        def turn(i, carry):
            start_copy(i).wait_send()
            return carry

        lax.fori_loop(0, GROUP, turn, 0)

    @pl.when(me + 1 < devices)
    def _():
        r_copy.wait_send()

    @pl.when(ahead_valid)
    def _():
        p_copy.wait_send()

    def end_e(other, carry):
        e_copy(other).wait_send()
        return carry

    lax.fori_loop(group + 1, groups, end_e, 0)


def shards(devices, initial, coarse_guess, feed_rate, kill_rate):
    rows, cols = initial.shape[1:]
    groups = devices // GROUP
    steps = (interval_time / STEPS_DEV, interval_time, interval_time * GROUP)
    tables = []
    for step in steps:
        tables += [jnp.asarray(table) for table in solve_tables(rows, cols, step)]
    state = (rows, 2 * cols)
    block = (1,) + initial.shape
    dma = pltpu.SemaphoreType.DMA
    whole = pl.BlockSpec(memory_space=pltpu.VMEM)
    return pl.pallas_call(
        functools.partial(kernel, devices, (rows, cols)),
        out_shape=[
            jax.ShapeDtypeStruct((STEPS_DEV,) + initial.shape, jnp.float32),
            jax.ShapeDtypeStruct(block, jnp.float32),
            jax.ShapeDtypeStruct(block, jnp.float32),
            jax.ShapeDtypeStruct(block, jnp.float32),
        ],
        in_specs=[whole] * (4 + len(tables)),
        out_specs=[whole] * 4,
        scratch_shapes=[
            pltpu.VMEM((6,) + state, jnp.float32),
            pltpu.VMEM((GROUP,) + state, jnp.float32),
            pltpu.VMEM(state, jnp.float32),
            pltpu.VMEM(state, jnp.float32),
            pltpu.VMEM(state, jnp.float32),
            pltpu.VMEM((groups,) + state, jnp.float32),
            pltpu.VMEM(state, jnp.float32),
            pltpu.VMEM(state, jnp.float32),
            pltpu.VMEM(state, jnp.float32),
            dma((GROUP,)),
            dma((GROUP,)),
            dma((GROUP,)),
            dma,
            dma,
            dma,
            dma,
            dma,
            dma((groups,)),
            dma((groups,)),
        ],
        compiler_params=pltpu.CompilerParams(collective_id=0, has_side_effects=True),
    )(initial, coarse_guess, feed_rate, kill_rate, *tables)


def solution(mesh):
    spread = P("tm", None, None, None)
    return jax.shard_map(
        functools.partial(shards, mesh.shape["tm"]),
        mesh=mesh,
        in_specs=(P(), spread, P(), P()),
        out_specs=(spread, spread, spread, spread),
        check_vma=False,
    )
```

time: 183 us -> 45 us (0.25)
  the two profiles are of different devices: /device:TPU:0 before, /device:TPU:31 now
where the time goes in v1:
time: 45 us; the launch traced here: 44.8 us
  Pallas kernels  40.1 us (89%)
  local copies, waits for them, and re-layouts  4.06 us (9%)
  between operations  0.65 us (1%)
    pallas_call x1, Pallas kernels, shards(): pl.pallas_call(functools.partial(kernel, devices, (rows, cols)), out_shap...  40.1 us
    unnamed x10, local copies, waits for them, and re-layouts  4.06 us

profile of v1, /device:TPU:31, one launch (start us, length us, event | category | flops | bytes accessed | tf_op | source)
XLA Modules:
  0.0 44.8 jit_solution(4590504700794527161)
XLA Ops:
  0.6 40.1 %shard_map.156 = (f32[4,2,64,64]{3,2,1,0:T(8,128)}, f32[1,2,64,64]{3,2,1,0:T(8,128)}, f32[1,2,64,64]{3,2,1,0:T(8,128)}, f32[1,2,64,64]{3,2,1,0:T(8,128)}) custom-call(f32[2,64,64]{2,1,0:T(8,128)} %refs_0_.1, f32[1,2,64,64]{3,2,1,0:T(8,128)} %refs_1_.1, f32[64,64]{1,0:T(8,128)} %refs_2_.1, f32[64,64]{1,0:T(8,128)} %refs_3_.1, ...), custom_call_target="tpu_custom_call" | custom-call | tf_op jit(solution)/shard_map/pallas_call | solution.py:390
  40.7 0.0 copy-start.2
  40.7 1.7 %copy.21 = f32[4,2,64,64]{3,2,1,0:T(8,128)} copy(f32[4,2,64,64]{3,2,1,0:T(8,128)} %get-tuple-element.8) | data formatting | bytes 262144
  42.4 0.0 copy-done.2
  42.4 0.0 copy-start.1
  42.4 0.6 %copy.22 = f32[1,2,64,64]{3,2,1,0:T(8,128)} copy(f32[1,2,64,64]{3,2,1,0:T(8,128)S(1)} %copy-done.2) | data formatting | bytes 65536
  43.1 0.2 copy-done.1
  43.3 0.0 copy-start
  43.3 0.6 %copy.23 = f32[1,2,64,64]{3,2,1,0:T(8,128)} copy(f32[1,2,64,64]{3,2,1,0:T(8,128)S(1)} %copy-done.1) | data formatting | bytes 65536
  43.9 0.2 copy-done
  44.2 0.6 %copy.24 = f32[1,2,64,64]{3,2,1,0:T(8,128)} copy(f32[1,2,64,64]{3,2,1,0:T(8,128)S(1)} %copy-done) | data formatting | bytes 65536
Async XLA Ops:
  40.7 1.7 %copy-start.2 = (f32[1,2,64,64]{3,2,1,0:T(8,128)S(1)}, f32[1,2,64,64]{3,2,1,0:T(8,128)}, u32[]{:S(2)}) copy-start(f32[1,2,64,64]{3,2,1,0:T(8,128)} %get-tuple-element.9) | copy-start | bytes 98308
  42.4 0.9 %copy-start.1 = (f32[1,2,64,64]{3,2,1,0:T(8,128)S(1)}, f32[1,2,64,64]{3,2,1,0:T(8,128)}, u32[]{:S(2)}) copy-start(f32[1,2,64,64]{3,2,1,0:T(8,128)} %get-tuple-element.10) | copy-start | bytes 98308
  43.3 0.9 %copy-start = (f32[1,2,64,64]{3,2,1,0:T(8,128)S(1)}, f32[1,2,64,64]{3,2,1,0:T(8,128)}, u32[]{:S(2)}) copy-start(f32[1,2,64,64]{3,2,1,0:T(8,128)} %get-tuple-element.11) | copy-start | bytes 98308

commit v2 on v1

--- a/solution.py
+++ b/solution.py
@@ -92,45 +92,55 @@
 def kernel(devices, sizes, *refs):
     (initial_ref, guess_ref, feed_ref, kill_ref) = refs[:4]
     table_refs = (refs[4:7], refs[7:10], refs[10:13])
-    traj_ref, resid_ref, coarse_ref, defect_ref = refs[13:17]
-    (rates, b_buf, s_buf, r_buf, p_buf, e_buf, b_out, r_out, p_out) = refs[17:26]
-    (send_b, recv_b, send_s, recv_s, send_r, recv_r, send_p, recv_p, send_e, recv_e) = refs[26:36]
+    packed_ref = refs[13]
+    (rates, b_buf, s_buf, r_buf, p_buf, e_buf, c_buf, b_out, r_out, s_out, p_out, c_out) = refs[14:26]
+    (send_b, recv_b, send_s, recv_s, send_r, recv_r, send_p, recv_p, send_e, recv_e, send_c, recv_c) = refs[26:38]
     rows, cols = sizes
     groups = devices // GROUP
     me = lax.axis_index("tm")
     group = me // GROUP
     member = me % GROUP
     base = group * GROUP
-    ahead = me + 2
-    ahead_group = ahead // GROUP
-    ahead_slot = ahead % GROUP
-    ahead_valid = ahead < devices
+    slot = (member + 2) % GROUP
+    wraps = member >= GROUP - 2
+    works = jnp.logical_or(group > 0, jnp.logical_not(wraps))
+    passes_guess = jnp.logical_and(wraps, group < groups - 1)
+    takes_guess = jnp.logical_and(wraps, group > 0)
+    sends_start = jnp.logical_and(group > 0, member == GROUP - 2)
+    sends_relaxed = jnp.logical_or(group > 0, member < GROUP - 1)
 
     barrier = pltpu.get_barrier_semaphore()
 
     def greet(other):
         pl.semaphore_signal(barrier, inc=1, device_id=(other,), device_id_type=MESH)
 
-    def greet_source(k, carry):
-        source = base + k - 2
-
-        @pl.when(jnp.logical_and(source >= 0, source != me))
-        def _():
-            greet(source)
-
+    def peer(i):
+        return base + (member + 1 + i) % GROUP
+
+    def greet_peer(i, carry):
+        greet(peer(i))
         return carry
-
-    lax.fori_loop(0, GROUP, greet_source, 0)
-
-    @pl.when(me >= 1)
-    def _():
-        greet(me - 1)
 
     def greet_group(other, carry):
         greet(other * GROUP + member)
         return carry
 
     lax.fori_loop(0, group, greet_group, 0)
+
+    @pl.when(takes_guess)
+    def _():
+        greet(me - GROUP)
+
+    lax.fori_loop(0, GROUP - 1, greet_peer, 0)
+
+    def await_barrier():
+        pl.semaphore_wait(barrier, GROUP - 1 + groups - 1 - group + jnp.where(passes_guess, 1, 0))
+
+    def remote(source, target, send, recv, other):
+        return pltpu.make_async_remote_copy(
+            src_ref=source, dst_ref=target, send_sem=send, recv_sem=recv,
+            device_id=(other,), device_id_type=MESH,
+        )
 
     left_half = lax.broadcasted_iota(jnp.int32, (rows, 2 * cols), 1) < cols
     fine_step = interval_time / STEPS_DEV
@@ -145,10 +155,6 @@
 
     def pack(ref):
         return jnp.concatenate([ref[0], ref[1]], axis=1)
-
-    def unpack(ref, index, value):
-        ref[index, 0] = value[:, :cols]
-        ref[index, 1] = value[:, cols:]
 
     def split(value):
         high = value.astype(jnp.bfloat16)
@@ -202,73 +208,71 @@
 
     start = pack(initial_ref)
     own = pack(guess_ref.at[0])
+    c_out[...] = own
+
+    @pl.when(jnp.logical_not(takes_guess))
+    def _():
+        c_buf[...] = own
+
+    guess_copy = remote(c_out, c_buf, send_c, recv_c, me + GROUP)
+
+    @pl.when(wraps)
+    def _():
+        await_barrier()
+
+    @pl.when(passes_guess)
+    def _():
+        guess_copy.start()
+
+    @pl.when(takes_guess)
+    def _():
+        remote(c_out, c_buf, send_c, recv_c, me).wait_recv()
 
     def fine_turn(unused, pair):
         return tuple(evolve(0, *pair))
 
-    relaxed, relaxed_zero = lax.fori_loop(0, STEPS_DEV, fine_turn, (own, start))
-    r_out[...] = relaxed
+    side = jnp.where(sends_start, own, start)
+    relaxed, relaxed_zero = lax.fori_loop(0, STEPS_DEV, fine_turn, (c_buf[...], side))
+    r_out[...] = jnp.where(sends_start, relaxed_zero, relaxed)
+    s_out[...] = relaxed
+
+    def s_copy(i):
+        return remote(s_out, s_buf, send_s.at[i], recv_s, peer(i))
+
+    def b_copy(i):
+        return remote(b_out, b_buf.at[slot], send_b.at[i], recv_b.at[slot], peer(i))
+
+    def over_peers(act):
+        def turn(i, carry):
+            act(i)
+            return carry
+
+        lax.fori_loop(0, GROUP - 1, turn, 0)
+
+    @pl.when(sends_start)
+    def _():
+        over_peers(lambda i: s_copy(i).start())
+
+    arrived, arrived_one = lax.fori_loop(0, STEPS_DEV, fine_turn, (relaxed, relaxed_zero))
     level_relaxed, level_relaxed_zero = evolve(1, relaxed, relaxed_zero)
-    arrived, arrived_one = lax.fori_loop(0, STEPS_DEV, fine_turn, (relaxed, relaxed_zero))
     p_out[...] = arrived
     b_out[...] = arrived - level_relaxed
-
-    targets = jnp.where(ahead_valid, GROUP - jnp.where(ahead_group == group, 1, 0), 0)
-    targets = targets + jnp.where(me + 1 < devices, 1, 0) + groups - 1 - group
-
-    @pl.when(targets > 0)
-    def _():
-        pl.semaphore_wait(barrier, targets)
-
-    def remote(source, target, send, recv, other):
-        return pltpu.make_async_remote_copy(
-            src_ref=source, dst_ref=target, send_sem=send, recv_sem=recv,
-            device_id=(other,), device_id_type=MESH,
-        )
-
-    def start_copy(i):
-        return remote(s_src, s_buf, send_s.at[i], recv_s, ahead_group * GROUP + i)
-
-    s_src = r_out
-
-    def b_copy(i):
-        return remote(b_out, b_buf.at[ahead_slot], send_b.at[i], recv_b.at[ahead_slot], ahead_group * GROUP + i)
-
-    sends_start = jnp.logical_and(ahead_valid, ahead_slot == 0)
-
-    def over_group(act):
-        def turn(i, carry):
-            @pl.when(jnp.logical_and(ahead_valid, ahead_group * GROUP + i != me))
-            def _():
-                act(i)
-
-            return carry
-
-        lax.fori_loop(0, GROUP, turn, 0)
-
-    @pl.when(sends_start)
-    def _():
-        def turn(i, carry):
-            start_copy(i).start()
-            return carry
-
-        lax.fori_loop(0, GROUP, turn, 0)
-
-    over_group(lambda i: b_copy(i).start())
-    r_copy = remote(r_out, r_buf, send_r, recv_r, me + 1)
-    p_copy = remote(p_out, p_buf, send_p, recv_p, me + 2)
-
-    @pl.when(me + 1 < devices)
+    r_copy = remote(r_out, r_buf, send_r, recv_r, base + (member + 1) % GROUP)
+    p_copy = remote(p_out, p_buf, send_p, recv_p, base + slot)
+
+    @pl.when(jnp.logical_not(wraps))
+    def _():
+        await_barrier()
+
+    @pl.when(works)
+    def _():
+        over_peers(lambda i: b_copy(i).start())
+        p_copy.start()
+        b_buf[slot] = b_out[...]
+
+    @pl.when(sends_relaxed)
     def _():
         r_copy.start()
-
-    @pl.when(ahead_valid)
-    def _():
-        p_copy.start()
-
-    @pl.when(jnp.logical_and(ahead_valid, ahead_group == group))
-    def _():
-        b_buf[ahead_slot] = b_out[...]
 
     @pl.when(group == 0)
     def _():
@@ -286,16 +290,18 @@
     def _():
         p_buf[...] = arrived_one
 
-    @pl.when(group > 0)
-    def _():
-        remote(r_out, s_buf, send_s.at[0], recv_s, me).wait_recv()
+    @pl.when(sends_start)
+    def _():
+        s_buf[...] = s_out[...]
+
+    @pl.when(jnp.logical_and(group > 0, jnp.logical_not(sends_start)))
+    def _():
+        remote(s_out, s_buf, send_s.at[0], recv_s, me).wait_recv()
 
     group_start = s_buf[...]
 
     def level_turn(k, state):
-        source = base + k - 2
-
-        @pl.when(jnp.logical_and(source >= 0, source != me))
+        @pl.when(jnp.logical_and(base + k >= 2, k != slot))
         def _():
             remote(b_out, b_buf.at[k], send_b.at[0], recv_b.at[k], me).wait_recv()
 
@@ -335,11 +341,11 @@
     point = prior
     for i in range(STEPS_DEV - 1):
         (point,) = evolve(0, point)
-        unpack(traj_ref, i, point)
+        packed_ref[i] = point
     last = member == GROUP - 1
-    unpack(traj_ref, STEPS_DEV - 1, jnp.where(last, mine, ending))
-    unpack(coarse_ref, 0, mine)
-    unpack(defect_ref, 0, jnp.where(last, ending - mine, 0.0))
+    packed_ref[STEPS_DEV - 1] = jnp.where(last, mine, ending)
+    packed_ref[STEPS_DEV + 1] = mine
+    packed_ref[STEPS_DEV + 2] = jnp.where(last, ending - mine, 0.0)
 
     @pl.when(me >= 1)
     def _():
@@ -349,31 +355,38 @@
     def _():
         remote(p_out, p_buf, send_p, recv_p, me).wait_recv()
 
-    unpack(resid_ref, 0, p_buf[...] - r_buf[...])
-
-    over_group(lambda i: b_copy(i).wait_send())
+    packed_ref[STEPS_DEV] = p_buf[...] - r_buf[...]
+
+    @pl.when(works)
+    def _():
+        over_peers(lambda i: b_copy(i).wait_send())
+        p_copy.wait_send()
 
     @pl.when(sends_start)
     def _():
-        def turn(i, carry):
-            start_copy(i).wait_send()
-            return carry
-
-        lax.fori_loop(0, GROUP, turn, 0)
-
-    @pl.when(me + 1 < devices)
+        over_peers(lambda i: s_copy(i).wait_send())
+
+    @pl.when(sends_relaxed)
     def _():
         r_copy.wait_send()
 
-    @pl.when(ahead_valid)
-    def _():
-        p_copy.wait_send()
+    @pl.when(passes_guess)
+    def _():
+        guess_copy.wait_send()
 
     def end_e(other, carry):
         e_copy(other).wait_send()
         return carry
 
     lax.fori_loop(group + 1, groups, end_e, 0)
+
+
+def unpack(packed_ref, traj_ref, resid_ref, coarse_ref, defect_ref):
+    cols = packed_ref.shape[2] // 2
+    places = [(traj_ref, i) for i in range(STEPS_DEV)] + [(resid_ref, 0), (coarse_ref, 0), (defect_ref, 0)]
+    for i, (ref, index) in enumerate(places):
+        ref[index, 0] = packed_ref[i, :, :cols]
+        ref[index, 1] = packed_ref[i, :, cols:]
 
 
 def shards(devices, initial, coarse_guess, feed_rate, kill_rate):
@@ -387,39 +400,37 @@
     block = (1,) + initial.shape
     dma = pltpu.SemaphoreType.DMA
     whole = pl.BlockSpec(memory_space=pltpu.VMEM)
+    buffer = pltpu.VMEM(state, jnp.float32)
+    packed = pl.pallas_call(
+        functools.partial(kernel, devices, (rows, cols)),
+        out_shape=jax.ShapeDtypeStruct((STEPS_DEV + 3,) + state, jnp.float32),
+        in_specs=[whole] * (4 + len(tables)),
+        out_specs=whole,
+        scratch_shapes=[
+            pltpu.VMEM((6,) + state, jnp.float32),
+            pltpu.VMEM((GROUP,) + state, jnp.float32),
+            buffer,
+            buffer,
+            buffer,
+            pltpu.VMEM((groups,) + state, jnp.float32),
+        ]
+        + [buffer] * 6
+        + [dma((GROUP,)), dma((GROUP,)), dma((GROUP,))]
+        + [dma] * 5
+        + [dma((groups,)), dma((groups,)), dma, dma],
+        compiler_params=pltpu.CompilerParams(collective_id=0, has_side_effects=True),
+    )(initial, coarse_guess, feed_rate, kill_rate, *tables)
     return pl.pallas_call(
-        functools.partial(kernel, devices, (rows, cols)),
+        unpack,
         out_shape=[
             jax.ShapeDtypeStruct((STEPS_DEV,) + initial.shape, jnp.float32),
             jax.ShapeDtypeStruct(block, jnp.float32),
             jax.ShapeDtypeStruct(block, jnp.float32),
             jax.ShapeDtypeStruct(block, jnp.float32),
         ],
-        in_specs=[whole] * (4 + len(tables)),
+        in_specs=[whole],
         out_specs=[whole] * 4,
-        scratch_shapes=[
-            pltpu.VMEM((6,) + state, jnp.float32),
-            pltpu.VMEM((GROUP,) + state, jnp.float32),
-            pltpu.VMEM(state, jnp.float32),
-            pltpu.VMEM(state, jnp.float32),
-            pltpu.VMEM(state, jnp.float32),
-            pltpu.VMEM((groups,) + state, jnp.float32),
-            pltpu.VMEM(state, jnp.float32),
-            pltpu.VMEM(state, jnp.float32),
-            pltpu.VMEM(state, jnp.float32),
-            dma((GROUP,)),
-            dma((GROUP,)),
-            dma((GROUP,)),
-            dma,
-            dma,
-            dma,
-            dma,
-            dma,
-            dma((groups,)),
-            dma((groups,)),
-        ],
-        compiler_params=pltpu.CompilerParams(collective_id=0, has_side_effects=True),
-    )(initial, coarse_guess, feed_rate, kill_rate, *tables)
+    )(packed)
 
 
 def solution(mesh):

time: 45 us -> 34.7 us (0.77)
  the two profiles are of different devices: /device:TPU:31 before, /device:TPU:23 now
where the time goes in v2:
time: 34.7 us; the launch traced here: 34.5 us
  Pallas kernels  33.8 us (97%)
  between operations  0.64 us (2%)
    pallas_call x1, Pallas kernels, shards(): pl.pallas_call(functools.partial(kernel, devices, (rows, cols)), out_shap...  32 us
    pallas_call x1, Pallas kernels, shards(): pl.pallas_call(unpack, out_shape=[jax.ShapeDtypeStruct((STEPS_DEV,) + ini...  1.8 us

profile of v2, /device:TPU:23, one launch (start us, length us, event | category | flops | bytes accessed | tf_op | source)
XLA Modules:
  0.0 34.5 jit_solution(605630783893843325)
XLA Ops:
  0.6 32.0 %shard_map.156.packed_ref = f32[7,64,128]{2,1,0:T(8,128)} custom-call(f32[2,64,64]{2,1,0:T(8,128)} %refs_0_.1, f32[1,2,64,64]{3,2,1,0:T(8,128)} %refs_1_.1, f32[64,64]{1,0:T(8,128)} %refs_2_.1, f32[64,64]{1,0:T(8,128)} %refs_3_.1, bf16[256,256]{1,0:T(8,128)(2,1)} %constant.18.clone.refs_4_, bf16[128,128]{1,0:T(8,128)(2,1)} %constant.19.clone.refs_5_, ...), custom_call_target="tpu_custom_call" | custom-call | tf_op jit(solution)/shard_map/pallas_call | solution.py:404
  32.7 1.8 %shard_map.157 = (f32[4,2,64,64]{3,2,1,0:T(8,128)}, f32[1,2,64,64]{3,2,1,0:T(8,128)}, f32[1,2,64,64]{3,2,1,0:T(8,128)}, f32[1,2,64,64]{3,2,1,0:T(8,128)}) custom-call(f32[7,64,128]{2,1,0:T(8,128)} %shard_map.156.packed_ref), custom_call_target="tpu_custom_call" | custom-call | tf_op jit(solution)/shard_map/pallas_call | solution.py:423

commit v3 on v2

--- a/solution.py
+++ b/solution.py
@@ -66,35 +66,32 @@
     rank = max(rank, 2)
     species = [factors(rows, cols, time_step, rate, rank) for rate in diffusion]
     short = rank == 2
-    blocks_high, blocks_low = [], []
-    for k in range(rank):
-        block = np.zeros((2 * cols, 2 * cols))
-        block[:cols, :cols] = species[0][1][k]
-        block[cols:, cols:] = species[1][1][k]
-        high, low = halves(block)
-        blocks_high.append(high)
-        blocks_low.append(low)
-    high = np.concatenate(blocks_high, 1)
-    right_high = np.concatenate([high, high], 0)
-    right_low = np.concatenate(blocks_low[: 1 if short else rank], 1)
-    left_high, left_low = [], []
-    for k in range(rank):
-        high, low = halves(np.concatenate([species[0][0][k], species[1][0][k]], 0))
-        left_high.append(high)
-        left_low.append(low)
-    if short:
-        lefts = left_high + left_high[:1] + left_low[:1]
-    else:
-        lefts = left_high + left_high + left_low
-    return right_high, right_low, np.concatenate(lefts, 1)
+    rights, lefts = [], []
+    for firsts, seconds in species:
+        highs, lows = [], []
+        for second in seconds:
+            high, low = halves(second)
+            highs += [high] * 2
+            lows += [low] * 2
+        high = np.concatenate(highs, 1)
+        low = np.concatenate(lows, 1)
+        rights.append(np.concatenate([high, high, low, np.zeros_like(low)], 0))
+        pairs = [halves(first) for first in firsts]
+        highs = [high for high, low in pairs]
+        lows = [low for high, low in pairs]
+        if short:
+            lefts.append(np.concatenate(highs + highs[:1] + lows[:1], 1))
+        else:
+            lefts.append(np.concatenate(highs + highs + lows, 1))
+    return np.stack(rights), np.stack(lefts)
 
 
 def kernel(devices, sizes, *refs):
     (initial_ref, guess_ref, feed_ref, kill_ref) = refs[:4]
-    table_refs = (refs[4:7], refs[7:10], refs[10:13])
-    packed_ref = refs[13]
-    (rates, b_buf, s_buf, r_buf, p_buf, e_buf, c_buf, b_out, r_out, s_out, p_out, c_out) = refs[14:26]
-    (send_b, recv_b, send_s, recv_s, send_r, recv_r, send_p, recv_p, send_e, recv_e, send_c, recv_c) = refs[26:38]
+    table_refs = (refs[4:6], refs[6:8], refs[8:10])
+    packed_ref = refs[10]
+    (rates, b_buf, s_buf, r_buf, p_buf, e_buf, c_buf, b_out, r_out, s_out, p_out, c_out) = refs[11:23]
+    (send_b, recv_b, send_s, recv_s, send_r, recv_r, send_p, recv_p, send_e, recv_e, send_c, recv_c) = refs[23:35]
     rows, cols = sizes
     groups = devices // GROUP
     me = lax.axis_index("tm")
@@ -147,14 +144,26 @@
     steps = (fine_step, interval_time, interval_time * GROUP)
     feed = jnp.concatenate([feed_ref[...]] * 2, axis=1)
     kill = jnp.concatenate([kill_ref[...]] * 2, axis=1)
-    source_term = jnp.where(left_half, feed, 0.0)
-    decay = jnp.where(left_half, feed, feed + kill)
     for level, step in enumerate(steps):
-        rates[2 * level] = 1.0 - step * decay
-        rates[2 * level + 1] = step * source_term
-
-    def pack(ref):
-        return jnp.concatenate([ref[0], ref[1]], axis=1)
+        rates[3 * level] = 1.0 - step * feed
+        rates[3 * level + 1] = step * feed
+        rates[3 * level + 2] = 1.0 - step * (feed + kill)
+
+    def double(value):
+        return jnp.concatenate([value, value], axis=1)
+
+    def join(state):
+        return jnp.where(left_half, state[0], state[1])
+
+    def spread(value):
+        turned = pltpu.roll(value, cols, 1)
+        return jnp.where(left_half, value, turned), jnp.where(left_half, turned, value)
+
+    def plus(state, other):
+        return state[0] + other[0], state[1] + other[1]
+
+    def minus(state, other):
+        return state[0] - other[0], state[1] - other[1]
 
     def split(value):
         high = value.astype(jnp.bfloat16)
@@ -164,31 +173,20 @@
     def dot(first, second):
         return jnp.dot(first, second, preferred_element_type=jnp.float32)
 
-    def evolve(level, *states):
-        step = steps[level]
-        right_high, right_low, lefts = table_refs[level]
-        terms = right_high.shape[1] // (2 * cols)
-        signed = jnp.where(left_half, -step, step)
-        reacted = []
-        for state in states:
-            swapped = pltpu.roll(state, cols, 1)
-            second = jnp.where(left_half, swapped, state)
-            uptake = state * swapped * second
-            reacted.append(rates[2 * level] * state + rates[2 * level + 1] + signed * uptake)
-        main = jnp.concatenate(reacted, 0) if len(reacted) > 1 else reacted[0]
-        high, low = split(main)
-        wide = dot(jnp.concatenate([high, low], 1), right_high[...])
-        narrow = dot(high, right_low[...])
-        parts = []
-        for k in range(terms):
-            part = wide[:, 2 * cols * k : 2 * cols * (k + 1)]
-            if 2 * cols * k < right_low.shape[1]:
-                part = part + narrow[:, 2 * cols * k : 2 * cols * (k + 1)]
-            parts.append(part)
+    def solve(level, kind, values):
+        rights, lefts = table_refs[level]
+        terms = rights.shape[2] // (2 * cols)
+        main = jnp.concatenate(values, 0) if len(values) > 1 else values[0]
+        mask = jnp.concatenate([left_half] * len(values), 0) if len(values) > 1 else left_half
+        high = main.astype(jnp.bfloat16)
+        wide = high.astype(jnp.float32)
+        mixed = jnp.where(mask, wide, main - wide).astype(jnp.bfloat16)
+        product = dot(jnp.concatenate([mixed, high], 1), rights[kind])
+        parts = [product[:, 2 * cols * k : 2 * cols * (k + 1)] for k in range(terms)]
         first = main + parts[0]
         parts[0] = first
         columns = []
-        for n in range(len(states)):
+        for n in range(len(values)):
             pieces = [part[rows * n : rows * (n + 1)] for part in parts]
             if terms == 2:
                 first_high, first_low = split(pieces[0])
@@ -198,21 +196,29 @@
                 stack = [a for a, b in pairs] + [b for a, b in pairs] + [a for a, b in pairs]
             columns.append(jnp.concatenate(stack, 0))
         stacked = jnp.concatenate(columns, 1) if len(columns) > 1 else columns[0]
-        product = dot(lefts[...], stacked)
-        finished = []
-        for n in range(len(states)):
-            piece = product[:, 2 * cols * n : 2 * cols * (n + 1)]
-            small = jnp.where(left_half, piece[:rows], piece[rows:])
-            finished.append(first[rows * n : rows * (n + 1)] + small)
-        return finished
-
-    start = pack(initial_ref)
-    own = pack(guess_ref.at[0])
-    c_out[...] = own
+        small = dot(lefts[kind], stacked)
+        return [
+            first[rows * n : rows * (n + 1)] + small[:, 2 * cols * n : 2 * cols * (n + 1)]
+            for n in range(len(values))
+        ]
+
+    def evolve(level, *states):
+        step = steps[level]
+        reacted = ([], [])
+        for substrate, catalyst in states:
+            uptake = step * (substrate * (catalyst * catalyst))
+            reacted[0].append(rates[3 * level] * substrate + rates[3 * level + 1] - uptake)
+            reacted[1].append(rates[3 * level + 2] * catalyst + uptake)
+        return list(zip(solve(level, 0, reacted[0]), solve(level, 1, reacted[1])))
+
+    start = double(initial_ref[0]), double(initial_ref[1])
+    own = double(guess_ref[0, 0]), double(guess_ref[0, 1])
+    own_packed = join(own)
+    c_out[...] = own_packed
 
     @pl.when(jnp.logical_not(takes_guess))
     def _():
-        c_buf[...] = own
+        c_buf[...] = own_packed
 
     guess_copy = remote(c_out, c_buf, send_c, recv_c, me + GROUP)
 
@@ -231,10 +237,12 @@
     def fine_turn(unused, pair):
         return tuple(evolve(0, *pair))
 
-    side = jnp.where(sends_start, own, start)
-    relaxed, relaxed_zero = lax.fori_loop(0, STEPS_DEV, fine_turn, (c_buf[...], side))
-    r_out[...] = jnp.where(sends_start, relaxed_zero, relaxed)
-    s_out[...] = relaxed
+    side = tuple(jnp.where(sends_start, mine, theirs) for mine, theirs in zip(own, start))
+    relaxed, relaxed_zero = lax.fori_loop(0, STEPS_DEV, fine_turn, (spread(c_buf[...]), side))
+    relaxed_packed = join(relaxed)
+    zero_packed = join(relaxed_zero)
+    r_out[...] = jnp.where(sends_start, zero_packed, relaxed_packed)
+    s_out[...] = relaxed_packed
 
     def s_copy(i):
         return remote(s_out, s_buf, send_s.at[i], recv_s, peer(i))
@@ -255,8 +263,8 @@
 
     arrived, arrived_one = lax.fori_loop(0, STEPS_DEV, fine_turn, (relaxed, relaxed_zero))
     level_relaxed, level_relaxed_zero = evolve(1, relaxed, relaxed_zero)
-    p_out[...] = arrived
-    b_out[...] = arrived - level_relaxed
+    p_out[...] = join(arrived)
+    b_out[...] = join(minus(arrived, level_relaxed))
     r_copy = remote(r_out, r_buf, send_r, recv_r, base + (member + 1) % GROUP)
     p_copy = remote(p_out, p_buf, send_p, recv_p, base + slot)
 
@@ -277,18 +285,18 @@
     @pl.when(group == 0)
     def _():
         (level_start,) = evolve(1, start)
-        s_buf[...] = start
-        b_buf[0] = relaxed_zero - level_start
-        b_buf[1] = arrived_one - level_relaxed_zero
+        s_buf[...] = join(start)
+        b_buf[0] = join(minus(relaxed_zero, level_start))
+        b_buf[1] = join(minus(arrived_one, level_relaxed_zero))
 
     @pl.when(me == 0)
     def _():
-        r_buf[...] = relaxed_zero
-        p_buf[...] = relaxed_zero
+        r_buf[...] = zero_packed
+        p_buf[...] = zero_packed
 
     @pl.when(me == 1)
     def _():
-        p_buf[...] = arrived_one
+        p_buf[...] = join(arrived_one)
 
     @pl.when(sends_start)
     def _():
@@ -298,7 +306,7 @@
     def _():
         remote(s_out, s_buf, send_s.at[0], recv_s, me).wait_recv()
 
-    group_start = s_buf[...]
+    group_start = spread(s_buf[...])
 
     def level_turn(k, state):
         @pl.when(jnp.logical_and(base + k >= 2, k != slot))
@@ -306,11 +314,13 @@
             remote(b_out, b_buf.at[k], send_b.at[0], recv_b.at[k], me).wait_recv()
 
         (state,) = evolve(1, state)
-        return state + b_buf[k]
+        return plus(state, spread(b_buf[k]))
 
     coarse_start, coarse_initial = evolve(2, group_start, start)
-    closing = lax.fori_loop(0, GROUP, level_turn, group_start)
-    e_buf[group] = closing - coarse_start
+    opens = group == 0
+    opening = tuple(jnp.where(opens, a, b) for a, b in zip(relaxed_zero, group_start))
+    closing = lax.fori_loop(jnp.where(opens, 1, 0), GROUP, level_turn, opening)
+    e_buf[group] = join(minus(closing, coarse_start))
 
     def e_copy(other):
         return remote(e_buf.at[group], e_buf.at[group], send_e.at[other], recv_e.at[group], other * GROUP + member)
@@ -321,27 +331,35 @@
 
     lax.fori_loop(group + 1, groups, start_e, 0)
 
-    def coarse_turn(other, pair):
-        before, image = pair
+    def await_e(other):
         remote(e_buf.at[other], e_buf.at[other], send_e.at[0], recv_e.at[other], me).wait_recv()
-        after = image + e_buf[other]
-        (image,) = evolve(2, after)
-        return after, image
-
-    earlier, image = lax.fori_loop(0, group, coarse_turn, (start, coarse_initial))
-    mine = image + e_buf[group]
+
+    def coarse_turn(other, before):
+        await_e(other)
+        (image,) = evolve(2, before)
+        return plus(image, spread(e_buf[other]))
+
+    @pl.when(group > 0)
+    def _():
+        await_e(0)
+
+    first_coarse = plus(coarse_initial, spread(e_buf[0]))
+    earlier = tuple(jnp.where(opens, a, b) for a, b in zip(start, first_coarse))
+    earlier = lax.fori_loop(1, group, coarse_turn, earlier)
 
     def replay(k, state):
         (state,) = evolve(1, state)
-        return state + b_buf[k]
+        return plus(state, spread(b_buf[k]))
 
     prior = lax.fori_loop(0, member, replay, earlier)
+    (mine,) = evolve(2, earlier)
+    mine = join(mine) + e_buf[group]
     (ending,) = evolve(1, prior)
-    ending = ending + b_buf[member]
+    ending = join(ending) + b_buf[member]
     point = prior
     for i in range(STEPS_DEV - 1):
         (point,) = evolve(0, point)
-        packed_ref[i] = point
+        packed_ref[i] = join(point)
     last = member == GROUP - 1
     packed_ref[STEPS_DEV - 1] = jnp.where(last, mine, ending)
     packed_ref[STEPS_DEV + 1] = mine
@@ -407,7 +425,7 @@
         in_specs=[whole] * (4 + len(tables)),
         out_specs=whole,
         scratch_shapes=[
-            pltpu.VMEM((6,) + state, jnp.float32),
+            pltpu.VMEM((9,) + state, jnp.float32),
             pltpu.VMEM((GROUP,) + state, jnp.float32),
             buffer,
             buffer,

time: 34.7 us -> 37.4 us (1.078)
  Pallas kernels: 33.8 us -> 36.6 us
    pallas_call x1, Pallas kernels: 32 us -> 34.8 us  [shards(): pl.pallas_call(functools.partial(kernel, devices, (rows, cols)), out_shap...]
where the time goes in v3:
time: 37.4 us; the launch traced here: 37.2 us
  Pallas kernels  36.6 us (98%)
  between operations  0.64 us (2%)
    pallas_call x1, Pallas kernels, shards(): pl.pallas_call(functools.partial(kernel, devices, (rows, cols)), out_shap...  34.8 us
    pallas_call x1, Pallas kernels, shards(): pl.pallas_call(unpack, out_shape=[jax.ShapeDtypeStruct((STEPS_DEV,) + ini...  1.8 us

profile of v3, /device:TPU:23, one launch (start us, length us, event | category | flops | bytes accessed | tf_op | source)
XLA Modules:
  0.0 37.2 jit_solution(3516613220334743401)
XLA Ops:
  0.6 34.8 %shard_map.129.packed_ref = f32[7,64,128]{2,1,0:T(8,128)} custom-call(f32[2,64,64]{2,1,0:T(8,128)} %refs_0_.1, f32[1,2,64,64]{3,2,1,0:T(8,128)} %refs_1_.1, f32[64,64]{1,0:T(8,128)} %refs_2_.1, f32[64,64]{1,0:T(8,128)} %refs_3_.1, bf16[2,256,256]{2,1,0:T(8,128)(2,1)} %constant.12.clone.refs_4_, bf16[2,64,256]{2,1,0:T(8,128)(2,1)} %constant.13.clone.refs_5_, ...), custom_call_target="tpu_custom_call" | custom-call | tf_op jit(solution)/shard_map/pallas_call | solution.py:422
  35.4 1.8 %shard_map.130 = (f32[4,2,64,64]{3,2,1,0:T(8,128)}, f32[1,2,64,64]{3,2,1,0:T(8,128)}, f32[1,2,64,64]{3,2,1,0:T(8,128)}, f32[1,2,64,64]{3,2,1,0:T(8,128)}) custom-call(f32[7,64,128]{2,1,0:T(8,128)} %shard_map.129.packed_ref), custom_call_target="tpu_custom_call" | custom-call | tf_op jit(solution)/shard_map/pallas_call | solution.py:441

commit v4 on v3

--- a/solution.py
+++ b/solution.py
@@ -173,20 +173,24 @@
     def dot(first, second):
         return jnp.dot(first, second, preferred_element_type=jnp.float32)
 
-    def solve(level, kind, values):
-        rights, lefts = table_refs[level]
-        terms = rights.shape[2] // (2 * cols)
-        main = jnp.concatenate(values, 0) if len(values) > 1 else values[0]
-        mask = jnp.concatenate([left_half] * len(values), 0) if len(values) > 1 else left_half
+    def stacked_rows(values):
+        return jnp.concatenate(values, 0) if len(values) > 1 else values[0]
+
+    def spectral(level, kind, main):
+        count = main.shape[0] // rows
         high = main.astype(jnp.bfloat16)
         wide = high.astype(jnp.float32)
-        mixed = jnp.where(mask, wide, main - wide).astype(jnp.bfloat16)
-        product = dot(jnp.concatenate([mixed, high], 1), rights[kind])
+        mixed = jnp.where(stacked_rows([left_half] * count), wide, main - wide).astype(jnp.bfloat16)
+        return dot(jnp.concatenate([mixed, high], 1), table_refs[level][0][kind])
+
+    def gather_terms(main, product):
+        count = main.shape[0] // rows
+        terms = product.shape[1] // (2 * cols)
         parts = [product[:, 2 * cols * k : 2 * cols * (k + 1)] for k in range(terms)]
         first = main + parts[0]
         parts[0] = first
         columns = []
-        for n in range(len(values)):
+        for n in range(count):
             pieces = [part[rows * n : rows * (n + 1)] for part in parts]
             if terms == 2:
                 first_high, first_low = split(pieces[0])
@@ -195,11 +199,16 @@
                 pairs = [split(piece) for piece in pieces]
                 stack = [a for a, b in pairs] + [b for a, b in pairs] + [a for a, b in pairs]
             columns.append(jnp.concatenate(stack, 0))
-        stacked = jnp.concatenate(columns, 1) if len(columns) > 1 else columns[0]
-        small = dot(lefts[kind], stacked)
+        return first, jnp.concatenate(columns, 1) if count > 1 else columns[0]
+
+    def solve(level, mains):
+        products = [spectral(level, kind, main) for kind, main in enumerate(mains)]
+        gathered = [gather_terms(main, product) for main, product in zip(mains, products)]
+        smalls = [dot(table_refs[level][1][kind], stack) for kind, (first, stack) in enumerate(gathered)]
+        count = mains[0].shape[0] // rows
         return [
-            first[rows * n : rows * (n + 1)] + small[:, 2 * cols * n : 2 * cols * (n + 1)]
-            for n in range(len(values))
+            [first[rows * n : rows * (n + 1)] + small[:, 2 * cols * n : 2 * cols * (n + 1)] for n in range(count)]
+            for (first, stack), small in zip(gathered, smalls)
         ]
 
     def evolve(level, *states):
@@ -209,7 +218,7 @@
             uptake = step * (substrate * (catalyst * catalyst))
             reacted[0].append(rates[3 * level] * substrate + rates[3 * level + 1] - uptake)
             reacted[1].append(rates[3 * level + 2] * catalyst + uptake)
-        return list(zip(solve(level, 0, reacted[0]), solve(level, 1, reacted[1])))
+        return list(zip(*solve(level, [stacked_rows(values) for values in reacted])))
 
     start = double(initial_ref[0]), double(initial_ref[1])
     own = double(guess_ref[0, 0]), double(guess_ref[0, 1])

time: 37.4 us -> 32.7 us (0.87)
  Pallas kernels: 36.6 us -> 31.9 us
    pallas_call x1, Pallas kernels: 34.8 us -> 30.1 us  [shards(): pl.pallas_call(functools.partial(kernel, devices, (rows, cols)), out_shap...]
where the time goes in v4:
time: 32.7 us; the launch traced here: 32.5 us
  Pallas kernels  31.9 us (98%)
  between operations  0.64 us (2%)
    pallas_call x1, Pallas kernels, shards(): pl.pallas_call(functools.partial(kernel, devices, (rows, cols)), out_shap...  30.1 us
    pallas_call x1, Pallas kernels, shards(): pl.pallas_call(unpack, out_shape=[jax.ShapeDtypeStruct((STEPS_DEV,) + ini...  1.8 us

profile of v4, /device:TPU:23, one launch (start us, length us, event | category | flops | bytes accessed | tf_op | source)
XLA Modules:
  0.0 32.5 jit_solution(32777972812188631)
XLA Ops:
  0.6 30.1 %shard_map.129.packed_ref = f32[7,64,128]{2,1,0:T(8,128)} custom-call(f32[2,64,64]{2,1,0:T(8,128)} %refs_0_.1, f32[1,2,64,64]{3,2,1,0:T(8,128)} %refs_1_.1, f32[64,64]{1,0:T(8,128)} %refs_2_.1, f32[64,64]{1,0:T(8,128)} %refs_3_.1, bf16[2,256,256]{2,1,0:T(8,128)(2,1)} %constant.12.clone.refs_4_, bf16[2,64,256]{2,1,0:T(8,128)(2,1)} %constant.13.clone.refs_5_, ...), custom_call_target="tpu_custom_call" | custom-call | tf_op jit(solution)/shard_map/pallas_call | solution.py:431
  30.7 1.8 %shard_map.130 = (f32[4,2,64,64]{3,2,1,0:T(8,128)}, f32[1,2,64,64]{3,2,1,0:T(8,128)}, f32[1,2,64,64]{3,2,1,0:T(8,128)}, f32[1,2,64,64]{3,2,1,0:T(8,128)}) custom-call(f32[7,64,128]{2,1,0:T(8,128)} %shard_map.129.packed_ref), custom_call_target="tpu_custom_call" | custom-call | tf_op jit(solution)/shard_map/pallas_call | solution.py:450

commit v5 on v4

--- a/solution.py
+++ b/solution.py
@@ -75,7 +75,7 @@
             lows += [low] * 2
         high = np.concatenate(highs, 1)
         low = np.concatenate(lows, 1)
-        rights.append(np.concatenate([high, high, low, np.zeros_like(low)], 0))
+        rights.append(np.concatenate([high, high, low], 0))
         pairs = [halves(first) for first in firsts]
         highs = [high for high, low in pairs]
         lows = [low for high, low in pairs]
@@ -90,8 +90,8 @@
     (initial_ref, guess_ref, feed_ref, kill_ref) = refs[:4]
     table_refs = (refs[4:6], refs[6:8], refs[8:10])
     packed_ref = refs[10]
-    (rates, b_buf, s_buf, r_buf, p_buf, e_buf, c_buf, b_out, r_out, s_out, p_out, c_out) = refs[11:23]
-    (send_b, recv_b, send_s, recv_s, send_r, recv_r, send_p, recv_p, send_e, recv_e, send_c, recv_c) = refs[23:35]
+    (rates, b_buf, s_buf, r_buf, p_buf, e_buf, b_out, r_out, p_out) = refs[11:20]
+    (send_b, recv_b, send_s, recv_s, send_r, recv_r, send_p, recv_p, send_e, recv_e, send_f, send_o) = refs[20:32]
     rows, cols = sizes
     groups = devices // GROUP
     me = lax.axis_index("tm")
@@ -100,11 +100,9 @@
     base = group * GROUP
     slot = (member + 2) % GROUP
     wraps = member >= GROUP - 2
-    works = jnp.logical_or(group > 0, jnp.logical_not(wraps))
-    passes_guess = jnp.logical_and(wraps, group < groups - 1)
-    takes_guess = jnp.logical_and(wraps, group > 0)
-    sends_start = jnp.logical_and(group > 0, member == GROUP - 2)
-    sends_relaxed = jnp.logical_or(group > 0, member < GROUP - 1)
+    forwards = jnp.logical_and(wraps, group < groups - 1)
+    relays = jnp.logical_and(wraps, group > 0)
+    first_wrap = member == GROUP - 2
 
     barrier = pltpu.get_barrier_semaphore()
 
@@ -124,14 +122,18 @@
 
     lax.fori_loop(0, group, greet_group, 0)
 
-    @pl.when(takes_guess)
-    def _():
-        greet(me - GROUP)
+    @pl.when(jnp.logical_and(group > 0, member <= 1))
+    def _():
+        greet(me - 2)
+
+    @pl.when(jnp.logical_and(group > 0, member == 0))
+    def _():
+        greet(me - 1)
 
     lax.fori_loop(0, GROUP - 1, greet_peer, 0)
 
     def await_barrier():
-        pl.semaphore_wait(barrier, GROUP - 1 + groups - 1 - group + jnp.where(passes_guess, 1, 0))
+        pl.semaphore_wait(barrier, GROUP - 1 + groups - 1 - group + jnp.where(forwards, member - (GROUP - 3), 0))
 
     def remote(source, target, send, recv, other):
         return pltpu.make_async_remote_copy(
@@ -181,7 +183,7 @@
         high = main.astype(jnp.bfloat16)
         wide = high.astype(jnp.float32)
         mixed = jnp.where(stacked_rows([left_half] * count), wide, main - wide).astype(jnp.bfloat16)
-        return dot(jnp.concatenate([mixed, high], 1), table_refs[level][0][kind])
+        return dot(jnp.concatenate([mixed, high[:, :cols]], 1), table_refs[level][0][kind])
 
     def gather_terms(main, product):
         count = main.shape[0] // rows
@@ -222,42 +224,13 @@
 
     start = double(initial_ref[0]), double(initial_ref[1])
     own = double(guess_ref[0, 0]), double(guess_ref[0, 1])
-    own_packed = join(own)
-    c_out[...] = own_packed
-
-    @pl.when(jnp.logical_not(takes_guess))
-    def _():
-        c_buf[...] = own_packed
-
-    guess_copy = remote(c_out, c_buf, send_c, recv_c, me + GROUP)
-
-    @pl.when(wraps)
-    def _():
-        await_barrier()
-
-    @pl.when(passes_guess)
-    def _():
-        guess_copy.start()
-
-    @pl.when(takes_guess)
-    def _():
-        remote(c_out, c_buf, send_c, recv_c, me).wait_recv()
 
     def fine_turn(unused, pair):
         return tuple(evolve(0, *pair))
 
-    side = tuple(jnp.where(sends_start, mine, theirs) for mine, theirs in zip(own, start))
-    relaxed, relaxed_zero = lax.fori_loop(0, STEPS_DEV, fine_turn, (spread(c_buf[...]), side))
-    relaxed_packed = join(relaxed)
+    relaxed, relaxed_zero = lax.fori_loop(0, STEPS_DEV, fine_turn, (own, start))
     zero_packed = join(relaxed_zero)
-    r_out[...] = jnp.where(sends_start, zero_packed, relaxed_packed)
-    s_out[...] = relaxed_packed
-
-    def s_copy(i):
-        return remote(s_out, s_buf, send_s.at[i], recv_s, peer(i))
-
-    def b_copy(i):
-        return remote(b_out, b_buf.at[slot], send_b.at[i], recv_b.at[slot], peer(i))
+    r_out[...] = join(relaxed)
 
     def over_peers(act):
         def turn(i, carry):
@@ -266,28 +239,44 @@
 
         lax.fori_loop(0, GROUP - 1, turn, 0)
 
-    @pl.when(sends_start)
-    def _():
-        over_peers(lambda i: s_copy(i).start())
-
     arrived, arrived_one = lax.fori_loop(0, STEPS_DEV, fine_turn, (relaxed, relaxed_zero))
     level_relaxed, level_relaxed_zero = evolve(1, relaxed, relaxed_zero)
     p_out[...] = join(arrived)
     b_out[...] = join(minus(arrived, level_relaxed))
-    r_copy = remote(r_out, r_buf, send_r, recv_r, base + (member + 1) % GROUP)
-    p_copy = remote(p_out, p_buf, send_p, recv_p, base + slot)
+    r_copy = remote(r_out, r_buf, send_r, recv_r, me + 1)
+    p_copy = remote(p_out, p_buf, send_p, recv_p, me + 2)
+    s_forward = remote(r_out, s_buf, send_o, recv_s, me + GROUP)
+    b_forward = remote(b_out, b_buf.at[slot], send_f, recv_b.at[slot], me + GROUP)
+
+    def b_copy(i):
+        return remote(b_out, b_buf.at[slot], send_b.at[i], recv_b.at[slot], peer(i))
+
+    def b_relay(i):
+        return remote(b_buf.at[slot], b_buf.at[slot], send_b.at[i], recv_b.at[slot], peer(i))
+
+    def s_relay(i):
+        return remote(s_buf, s_buf, send_s.at[i], recv_s, peer(i))
+
+    await_barrier()
+
+    @pl.when(jnp.logical_and(forwards, first_wrap))
+    def _():
+        s_forward.start()
+
+    @pl.when(forwards)
+    def _():
+        b_forward.start()
 
     @pl.when(jnp.logical_not(wraps))
     def _():
-        await_barrier()
-
-    @pl.when(works)
-    def _():
         over_peers(lambda i: b_copy(i).start())
+        b_buf[slot] = b_out[...]
+
+    @pl.when(me + 2 < devices)
+    def _():
         p_copy.start()
-        b_buf[slot] = b_out[...]
-
-    @pl.when(sends_relaxed)
+
+    @pl.when(me + 1 < devices)
     def _():
         r_copy.start()
 
@@ -307,13 +296,18 @@
     def _():
         p_buf[...] = join(arrived_one)
 
-    @pl.when(sends_start)
-    def _():
-        s_buf[...] = s_out[...]
-
-    @pl.when(jnp.logical_and(group > 0, jnp.logical_not(sends_start)))
-    def _():
-        remote(s_out, s_buf, send_s.at[0], recv_s, me).wait_recv()
+    @pl.when(group > 0)
+    def _():
+        remote(r_out, s_buf, send_o, recv_s, me).wait_recv()
+
+    @pl.when(jnp.logical_and(relays, first_wrap))
+    def _():
+        over_peers(lambda i: s_relay(i).start())
+
+    @pl.when(relays)
+    def _():
+        b_forward.wait_recv()
+        over_peers(lambda i: b_relay(i).start())
 
     group_start = spread(s_buf[...])
 
@@ -384,22 +378,33 @@
 
     packed_ref[STEPS_DEV] = p_buf[...] - r_buf[...]
 
-    @pl.when(works)
+    @pl.when(jnp.logical_not(wraps))
     def _():
         over_peers(lambda i: b_copy(i).wait_send())
+
+    @pl.when(relays)
+    def _():
+        over_peers(lambda i: b_relay(i).wait_send())
+
+    @pl.when(jnp.logical_and(relays, first_wrap))
+    def _():
+        over_peers(lambda i: s_relay(i).wait_send())
+
+    @pl.when(jnp.logical_and(forwards, first_wrap))
+    def _():
+        s_forward.wait_send()
+
+    @pl.when(forwards)
+    def _():
+        b_forward.wait_send()
+
+    @pl.when(me + 2 < devices)
+    def _():
         p_copy.wait_send()
 
-    @pl.when(sends_start)
-    def _():
-        over_peers(lambda i: s_copy(i).wait_send())
-
-    @pl.when(sends_relaxed)
+    @pl.when(me + 1 < devices)
     def _():
         r_copy.wait_send()
-
-    @pl.when(passes_guess)
-    def _():
-        guess_copy.wait_send()
 
     def end_e(other, carry):
         e_copy(other).wait_send()
@@ -441,7 +446,7 @@
             buffer,
             pltpu.VMEM((groups,) + state, jnp.float32),
         ]
-        + [buffer] * 6
+        + [buffer] * 3
         + [dma((GROUP,)), dma((GROUP,)), dma((GROUP,))]
         + [dma] * 5
         + [dma((groups,)), dma((groups,)), dma, dma],

time: 32.7 us -> 31.4 us (0.960)
  Pallas kernels: 31.9 us -> 30.6 us
    pallas_call x1, Pallas kernels: 30.1 us -> 28.8 us  [shards(): pl.pallas_call(functools.partial(kernel, devices, (rows, cols)), out_shap...]
where the time goes in v5:
time: 31.4 us; the launch traced here: 31.3 us
  Pallas kernels  30.6 us (97%)
  between operations  0.64 us (2%)
    pallas_call x1, Pallas kernels, shards(): pl.pallas_call(functools.partial(kernel, devices, (rows, cols)), out_shap...  28.8 us
    pallas_call x1, Pallas kernels, shards(): pl.pallas_call(unpack, out_shape=[jax.ShapeDtypeStruct((STEPS_DEV,) + ini...  1.8 us

profile of v5, /device:TPU:23, one launch (start us, length us, event | category | flops | bytes accessed | tf_op | source)
XLA Modules:
  0.0 31.3 jit_solution(9907492858004783289)
XLA Ops:
  0.6 28.8 %shard_map.129.packed_ref = f32[7,64,128]{2,1,0:T(8,128)} custom-call(f32[2,64,64]{2,1,0:T(8,128)} %refs_0_.1, f32[1,2,64,64]{3,2,1,0:T(8,128)} %refs_1_.1, f32[64,64]{1,0:T(8,128)} %refs_2_.1, f32[64,64]{1,0:T(8,128)} %refs_3_.1, bf16[2,192,256]{2,1,0:T(8,128)(2,1)} %constant.12.clone.refs_4_, bf16[2,64,256]{2,1,0:T(8,128)(2,1)} %constant.13.clone.refs_5_, ...), custom_call_target="tpu_custom_call" | custom-call | tf_op jit(solution)/shard_map/pallas_call | solution.py:436
  29.5 1.8 %shard_map.130 = (f32[4,2,64,64]{3,2,1,0:T(8,128)}, f32[1,2,64,64]{3,2,1,0:T(8,128)}, f32[1,2,64,64]{3,2,1,0:T(8,128)}, f32[1,2,64,64]{3,2,1,0:T(8,128)}) custom-call(f32[7,64,128]{2,1,0:T(8,128)} %shard_map.129.packed_ref), custom_call_target="tpu_custom_call" | custom-call | tf_op jit(solution)/shard_map/pallas_call | solution.py:455

commit v6 on v5

--- a/solution.py
+++ b/solution.py
@@ -11,6 +11,7 @@
 
 STEPS_DEV = 4
 GROUP = 16
+CHUNK = 5
 
 diffusion = (0.2, 0.1)
 interval_time = 0.03125
@@ -228,7 +229,7 @@
     def fine_turn(unused, pair):
         return tuple(evolve(0, *pair))
 
-    relaxed, relaxed_zero = lax.fori_loop(0, STEPS_DEV, fine_turn, (own, start))
+    relaxed, relaxed_zero = lax.fori_loop(0, STEPS_DEV, fine_turn, (own, start), unroll=True)
     zero_packed = join(relaxed_zero)
     r_out[...] = join(relaxed)
 
@@ -239,7 +240,7 @@
 
         lax.fori_loop(0, GROUP - 1, turn, 0)
 
-    arrived, arrived_one = lax.fori_loop(0, STEPS_DEV, fine_turn, (relaxed, relaxed_zero))
+    arrived, arrived_one = lax.fori_loop(0, STEPS_DEV, fine_turn, (relaxed, relaxed_zero), unroll=True)
     level_relaxed, level_relaxed_zero = evolve(1, relaxed, relaxed_zero)
     p_out[...] = join(arrived)
     b_out[...] = join(minus(arrived, level_relaxed))
@@ -311,18 +312,29 @@
 
     group_start = spread(s_buf[...])
 
-    def level_turn(k, state):
+    def await_b(k):
         @pl.when(jnp.logical_and(base + k >= 2, k != slot))
         def _():
             remote(b_out, b_buf.at[k], send_b.at[0], recv_b.at[k], me).wait_recv()
 
+    def level_turn(k, state):
         (state,) = evolve(1, state)
         return plus(state, spread(b_buf[k]))
 
+    def level_chunk(n, state):
+        for i in range(CHUNK):
+            await_b(1 + n * CHUNK + i)
+        for i in range(CHUNK):
+            state = level_turn(1 + n * CHUNK + i, state)
+        return state
+
     coarse_start, coarse_initial = evolve(2, group_start, start)
     opens = group == 0
-    opening = tuple(jnp.where(opens, a, b) for a, b in zip(relaxed_zero, group_start))
-    closing = lax.fori_loop(jnp.where(opens, 1, 0), GROUP, level_turn, opening)
+    await_b(0)
+    opening = tuple(
+        jnp.where(opens, a, b) for a, b in zip(relaxed_zero, level_turn(0, group_start))
+    )
+    closing = lax.fori_loop(0, (GROUP - 1) // CHUNK, level_chunk, opening)
     e_buf[group] = join(minus(closing, coarse_start))
 
     def e_copy(other):
@@ -350,11 +362,14 @@
     earlier = tuple(jnp.where(opens, a, b) for a, b in zip(start, first_coarse))
     earlier = lax.fori_loop(1, group, coarse_turn, earlier)
 
-    def replay(k, state):
-        (state,) = evolve(1, state)
-        return plus(state, spread(b_buf[k]))
-
-    prior = lax.fori_loop(0, member, replay, earlier)
+    def replay_chunk(n, state):
+        for i in range(CHUNK):
+            state = level_turn(n * CHUNK + i, state)
+        return state
+
+    chunks = member // CHUNK
+    prior = lax.fori_loop(0, chunks, replay_chunk, earlier)
+    prior = lax.fori_loop(chunks * CHUNK, member, level_turn, prior)
     (mine,) = evolve(2, earlier)
     mine = join(mine) + e_buf[group]
     (ending,) = evolve(1, prior)
@@ -419,6 +434,9 @@
     for i, (ref, index) in enumerate(places):
         ref[index, 0] = packed_ref[i, :, :cols]
         ref[index, 1] = packed_ref[i, :, cols:]
+
+
+assert (GROUP - 1) % CHUNK == 0
 
 
 def shards(devices, initial, coarse_guess, feed_rate, kill_rate):

time: 31.4 us -> 30.7 us (0.978)
  Pallas kernels: 30.6 us -> 29.9 us
    pallas_call x1, Pallas kernels: 28.8 us -> 28.1 us  [shards(): pl.pallas_call(functools.partial(kernel, devices, (rows, cols)), out_shap...]
where the time goes in v6:
time: 30.7 us; the launch traced here: 30.6 us
  Pallas kernels  29.9 us (97%)
  between operations  0.64 us (2%)
    pallas_call x1, Pallas kernels, shards(): pl.pallas_call(functools.partial(kernel, devices, (rows, cols)), out_shap...  28.1 us
    pallas_call x1, Pallas kernels, shards(): pl.pallas_call(unpack, out_shape=[jax.ShapeDtypeStruct((STEPS_DEV,) + ini...  1.8 us

profile of v6, /device:TPU:23, one launch (start us, length us, event | category | flops | bytes accessed | tf_op | source)
XLA Modules:
  0.0 30.6 jit_solution(16292006452111715297)
XLA Ops:
  0.6 28.1 %shard_map.129.packed_ref = f32[7,64,128]{2,1,0:T(8,128)} custom-call(f32[2,64,64]{2,1,0:T(8,128)} %refs_0_.1, f32[1,2,64,64]{3,2,1,0:T(8,128)} %refs_1_.1, f32[64,64]{1,0:T(8,128)} %refs_2_.1, f32[64,64]{1,0:T(8,128)} %refs_3_.1, bf16[2,192,256]{2,1,0:T(8,128)(2,1)} %constant.12.clone.refs_4_, bf16[2,64,256]{2,1,0:T(8,128)(2,1)} %constant.13.clone.refs_5_, ...), custom_call_target="tpu_custom_call" | custom-call | tf_op jit(solution)/shard_map/pallas_call | solution.py:454
  28.8 1.8 %shard_map.130 = (f32[4,2,64,64]{3,2,1,0:T(8,128)}, f32[1,2,64,64]{3,2,1,0:T(8,128)}, f32[1,2,64,64]{3,2,1,0:T(8,128)}, f32[1,2,64,64]{3,2,1,0:T(8,128)}) custom-call(f32[7,64,128]{2,1,0:T(8,128)} %shard_map.129.packed_ref), custom_call_target="tpu_custom_call" | custom-call | tf_op jit(solution)/shard_map/pallas_call | solution.py:473
